TPU v7x, 32 devices: a whole 2x2x4 slice. The times are simulated.
32 devices in a mesh: dp: 16 (over z, y, x), rep: 2 (over core).
Axes of the slice: x: 2, y: 2, z: 4, core: 2. Of those that a mesh axis runs over, the one named last changes fastest.
Arguments:
- images: bfloat16 [1024, 145, 768], P(('dp', 'rep')), may hold values from -6 to 6
- groups: int32 [1024], P(('dp', 'rep')), may hold values from 0 to 1, as said below
- captions: bfloat16 [1024, 16, 768], P(('dp', 'rep')), may hold values from -6 to 6
- cap_lengths: int32 [1024], P(('dp', 'rep')), may hold values from 4 to 16, as said below
- img_gain_a: bfloat16 [768], P('rep'), may hold values from 0.5 to 1.5
- img_w_qkv: bfloat16 [768, 2304], P('rep'), may hold values from -0.21875 to 0.21875
- img_b_qv: bfloat16 [1536], P('rep'), may hold values from -3 to 3
- img_w_out: bfloat16 [768, 768], P('rep'), may hold values from -0.625 to 0.625
- img_gain_m: bfloat16 [768], P('rep'), may hold values from 0.5 to 1.5
- img_w_up: bfloat16 [768, 3072], P('rep'), may hold values from -0.21875 to 0.21875
- img_b_up: bfloat16 [3072], P('rep'), may hold values from -3 to 3
- img_w_down: bfloat16 [3072, 768], P('rep'), may hold values from -0.109375 to 0.109375
- gain_attn: bfloat16 [768], replicated, may hold values from 0.5 to 1.5
- w_qkv: bfloat16 [768, 2304], replicated, may hold values from -0.21875 to 0.21875
- b_qv: bfloat16 [1536], replicated, may hold values from -3 to 3
- w_out: bfloat16 [768, 768], replicated, may hold values from -0.625 to 0.625
- gain_mlp: bfloat16 [768], replicated, may hold values from 0.5 to 1.5
- w_up: bfloat16 [768, 3072], replicated, may hold values from -0.21875 to 0.21875
- b_up: bfloat16 [3072], replicated, may hold values from -3 to 3
- w_down: bfloat16 [3072, 768], replicated, may hold values from -0.109375 to 0.109375
- text_proj: bfloat16 [768, 768], replicated, may hold values from -0.21875 to 0.21875
Outputs:
- pair_loss: float32 [1024], P(('dp', 'rep'))
- caption_grad: float32 [1024, 16, 768], P(('dp', 'rep'))
- grad_gain_attn: float32 [768], P('rep')
- grad_w_qkv: float32 [768, 2304], P(None, 'rep')
- grad_b_qv: float32 [1536], P('rep')
- grad_w_out: float32 [768, 768], P(None, 'rep')
- grad_gain_mlp: float32 [768], P('rep')
- grad_w_up: float32 [768, 3072], P(None, 'rep')
- grad_b_up: float32 [3072], P('rep')
- grad_w_down: float32 [3072, 768], P(None, 'rep')
Inputs may be any that keep to these rules, and one draw needn't show every extreme that they name: `groups`: 1 marks an image of 145 tokens, 0 one of 50 tokens whose later positions are unused; the 32 pairs of every device hold images of both kinds. Positions of a caption from cap_lengths on are padding; the 32 pairs of every device hold a caption of 16 tokens.
All inputs are finite; a program needn't handle non-finite values.
Results may differ from a plain program's by a relative error of at most 0.0165.
Values may be sent and summed in bfloat16 or wider, within the bound.
No kernel may reach another device: no remote copies, remote signals or barrier semaphores. Data moves between devices by JAX's collectives and lax.ppermute only.
A program may use at most 192 MiB of HBM per device.

v0:
```python
import math

import jax
import jax.numpy as jnp
from jax import lax
from jax.sharding import PartitionSpec as P

D = 768
HEADS = 12
ILEN = 145
LOWLEN = 50
CAP = 16
IMG_BLK = 4


SCALE = 100.0
EPS = 1e-06
NEGATIVE = -1e30


def contract(left_side, right_side, left_dim, right_dim):
    return lax.dot_general(
        left_side,
        right_side,
        (((left_dim,), (right_dim,)), ((), ())),
        preferred_element_type=jnp.float32,
    )


def normalize(values):
    center = values - jnp.mean(values, -1, keepdims=True)
    inverse = lax.rsqrt(jnp.mean(center * center, -1, keepdims=True) + EPS)
    return (center * inverse, inverse)


def norm_back(grad_normed, normed, inverse):
    return inverse * (
        grad_normed
        - jnp.mean(grad_normed, -1, keepdims=True)
        - normed * jnp.mean(grad_normed * normed, -1, keepdims=True)
    )


def gelu_slope(values):
    return 0.5 * (1.0 + jax.scipy.special.erf(values / math.sqrt(2.0))) + values * jnp.exp(
        -0.5 * values * values
    ) / math.sqrt(2.0 * math.pi)


def block_forward(tokens, length, params):
    gain_a, weight_qkv, bias_qv, weight_out, gain_m, weight_up, bias_up, weight_down = params
    number, span_len, model_dim = tokens.shape
    head_dim = model_dim // HEADS
    scale_q = 1.0 / math.sqrt(head_dim)
    flat_rows = tokens.reshape(number * span_len, model_dim).astype(jnp.float32)
    normed_one, inverse_one = normalize(flat_rows)
    input_low = (normed_one * gain_a.astype(jnp.float32)).astype(jnp.bfloat16)
    bias_full = jnp.concatenate(
        [
            bias_qv[:model_dim].astype(jnp.float32),
            jnp.zeros((model_dim,), jnp.float32),
            bias_qv[model_dim:].astype(jnp.float32),
        ]
    )
    projected = (
        jnp.dot(input_low, weight_qkv, preferred_element_type=jnp.float32) + bias_full
    ).astype(jnp.bfloat16)
    projected = projected.reshape(number, span_len, 3, HEADS, head_dim)
    query_rows = projected[:, :, 0]
    key_rows = projected[:, :, 1]
    value_rows = projected[:, :, 2]
    valid_key = jnp.arange(span_len, dtype=jnp.int32)[None, :] < length[:, None]
    scores = (
        jnp.einsum("bqhd,bkhd->bhqk", query_rows, key_rows, preferred_element_type=jnp.float32)
        * scale_q
    )
    scores = jnp.where(valid_key[:, None, None, :], scores, NEGATIVE)
    maxima = jnp.max(scores, -1, keepdims=True)
    powers = jnp.exp(scores - maxima)
    attention = powers / jnp.sum(powers, -1, keepdims=True)
    attn_low = attention.astype(jnp.bfloat16)
    mixed_heads = (
        jnp.einsum("bhqk,bkhd->bqhd", attn_low, value_rows, preferred_element_type=jnp.float32)
        .astype(jnp.bfloat16)
        .reshape(number * span_len, model_dim)
    )
    after_attn = flat_rows + jnp.dot(mixed_heads, weight_out, preferred_element_type=jnp.float32)
    normed_two, inverse_two = normalize(after_attn)
    mlp_in = (normed_two * gain_m.astype(jnp.float32)).astype(jnp.bfloat16)
    pre_act = jnp.dot(mlp_in, weight_up, preferred_element_type=jnp.float32) + bias_up.astype(
        jnp.float32
    )
    hidden = jax.nn.gelu(pre_act, approximate=False).astype(jnp.bfloat16)
    result = after_attn + jnp.dot(hidden, weight_down, preferred_element_type=jnp.float32)
    valid_mask = valid_key.astype(jnp.float32)[:, :, None]
    pooled = (
        jnp.sum(result.reshape(number, span_len, model_dim) * valid_mask, 1)
        / length.astype(jnp.float32)[:, None]
    )
    saved = (
        normed_one,
        inverse_one,
        input_low,
        query_rows,
        key_rows,
        value_rows,
        attention,
        attn_low,
        mixed_heads,
        normed_two,
        inverse_two,
        mlp_in,
        pre_act,
        hidden,
        valid_key,
    )
    return (pooled, saved)


def image_embed(pixels, length, params):
    pooled, saved = block_forward(pixels, length, params)
    return (pooled * lax.rsqrt(jnp.sum(pooled * pooled, -1, keepdims=True) + EPS)).astype(
        jnp.bfloat16
    )


def half_softmax(scores, own_pair):
    maxima = jnp.max(scores, -1, keepdims=True)
    powers = jnp.exp(scores - maxima)
    totals = jnp.sum(powers, -1, keepdims=True)
    log_total = maxima[:, 0] + jnp.log(totals[:, 0])
    loss_part = log_total - jnp.sum(scores * own_pair, -1)
    grad_part = (0.5 * (powers / totals - own_pair)).astype(jnp.bfloat16)
    return (loss_part, grad_part, log_total)


def local(
    images,
    groups,
    captions,
    cap_lengths,
    img_gain_a,
    img_w_qkv,
    img_b_qv,
    img_w_out,
    img_gain_m,
    img_w_up,
    img_b_up,
    img_w_down,
    gain_attn,
    w_qkv,
    b_qv,
    w_out,
    gain_mlp,
    w_up,
    b_up,
    w_down,
    text_proj,
):
    frozen = (
        lax.all_gather(img_gain_a, "rep", axis=0, tiled=True),
        lax.all_gather(img_w_qkv, "rep", axis=0, tiled=True),
        lax.all_gather(img_b_qv, "rep", axis=0, tiled=True),
        lax.all_gather(img_w_out, "rep", axis=0, tiled=True),
        lax.all_gather(img_gain_m, "rep", axis=0, tiled=True),
        lax.all_gather(img_w_up, "rep", axis=0, tiled=True),
        lax.all_gather(img_b_up, "rep", axis=0, tiled=True),
        lax.all_gather(img_w_down, "rep", axis=0, tiled=True),
    )
    local_pairs = images.shape[0]
    ordering = jnp.argsort(groups, stable=True)
    sorted_len = jnp.where(groups[ordering] == 1, ILEN, LOWLEN).astype(jnp.int32)
    blocks = local_pairs // IMG_BLK
    stacked = images[ordering].reshape(blocks, IMG_BLK, ILEN, D)

    def image_block(block_item):
        pixels, length = block_item
        return lax.cond(
            jnp.max(length) > LOWLEN,
            lambda: image_embed(pixels, length, frozen),
            lambda: image_embed(pixels[:, :LOWLEN], length, frozen),
        )

    sorted_emb = lax.map(image_block, (stacked, sorted_len.reshape(blocks, IMG_BLK))).reshape(
        local_pairs, D
    )
    image_emb = sorted_emb[jnp.argsort(ordering)]
    params = (gain_attn, w_qkv, b_qv, w_out, gain_mlp, w_up, b_up, w_down)
    pooled, saved = block_forward(captions, cap_lengths, params)
    (
        normed_one,
        inverse_one,
        input_low,
        query_rows,
        key_rows,
        value_rows,
        attention,
        attn_low,
        mixed_heads,
        normed_two,
        inverse_two,
        mlp_in,
        pre_act,
        hidden,
        valid_key,
    ) = saved
    proj_out = jnp.dot(pooled.astype(jnp.bfloat16), text_proj, preferred_element_type=jnp.float32)
    inverse_z = lax.rsqrt(jnp.sum(proj_out * proj_out, -1, keepdims=True) + EPS)
    unit_text = proj_out * inverse_z
    text_emb = unit_text.astype(jnp.bfloat16)
    all_text, all_image = (
        lax.all_gather(text_emb, ("dp", "rep"), axis=0, tiled=True),
        lax.all_gather(image_emb, ("dp", "rep"), axis=0, tiled=True),
    )
    total_pairs = all_text.shape[0]
    first_row = lax.axis_index(("dp", "rep")) * local_pairs
    own_pair = (
        jnp.arange(total_pairs, dtype=jnp.int32)[None, :]
        == first_row + jnp.arange(local_pairs, dtype=jnp.int32)[:, None]
    ).astype(jnp.float32)
    text_scores = contract(text_emb, all_image, 1, 1) * SCALE
    image_scores = contract(image_emb, all_text, 1, 1) * SCALE
    text_loss, text_sgrad, text_total = half_softmax(text_scores, own_pair)
    image_loss, image_sgrad, image_total = half_softmax(image_scores, own_pair)
    pair_loss = 0.5 * text_loss + 0.5 * image_loss
    row_part = contract(text_sgrad, all_image, 1, 0) * SCALE
    column_part = lax.psum_scatter(
        contract(image_sgrad, image_emb, 0, 0) * SCALE,
        ("dp", "rep"),
        scatter_dimension=0,
        tiled=True,
    )
    grad_unit = row_part + column_part
    grad_projout = (
        inverse_z * (grad_unit - unit_text * jnp.sum(unit_text * grad_unit, -1, keepdims=True))
    ).astype(jnp.bfloat16)
    grad_pooled = contract(grad_projout, text_proj, 1, 1)
    rows_total = local_pairs * CAP
    grad_rows = (
        (grad_pooled / cap_lengths.astype(jnp.float32)[:, None])[:, None, :]
        * valid_key.astype(jnp.float32)[:, :, None]
    ).reshape(rows_total, D)
    grad_branch = grad_rows.astype(jnp.bfloat16)
    grad_w_down = contract(hidden, grad_branch, 0, 0)
    grad_hidden = contract(grad_branch, w_down, 1, 1)
    grad_pre = (grad_hidden * gelu_slope(pre_act)).astype(jnp.bfloat16)
    grad_b_up = jnp.sum(grad_pre.astype(jnp.float32), 0)
    grad_w_up = contract(mlp_in, grad_pre, 0, 0)
    grad_mlp_in = contract(grad_pre, w_up, 1, 1)
    grad_gain_mlp = jnp.sum(grad_mlp_in * normed_two, 0)
    grad_after = grad_rows + norm_back(
        grad_mlp_in * gain_mlp.astype(jnp.float32), normed_two, inverse_two
    )
    grad_out_low = grad_after.astype(jnp.bfloat16)
    grad_w_out = contract(mixed_heads, grad_out_low, 0, 0)
    head_dim = D // HEADS
    scale_q = 1.0 / math.sqrt(head_dim)
    grad_mixed = (
        contract(grad_out_low, w_out, 1, 1)
        .astype(jnp.bfloat16)
        .reshape(local_pairs, CAP, HEADS, head_dim)
    )
    grad_attention = jnp.einsum(
        "bqhd,bkhd->bhqk", grad_mixed, value_rows, preferred_element_type=jnp.float32
    )
    grad_value = jnp.einsum(
        "bhqk,bqhd->bkhd", attn_low, grad_mixed, preferred_element_type=jnp.float32
    )
    grad_scores = (
        attention * (grad_attention - jnp.sum(grad_attention * attention, -1, keepdims=True))
    ).astype(jnp.bfloat16)
    grad_query = (
        jnp.einsum("bhqk,bkhd->bqhd", grad_scores, key_rows, preferred_element_type=jnp.float32)
        * scale_q
    )
    grad_key = (
        jnp.einsum("bhqk,bqhd->bkhd", grad_scores, query_rows, preferred_element_type=jnp.float32)
        * scale_q
    )
    grad_projected = (
        jnp.stack([grad_query, grad_key, grad_value], 2)
        .reshape(rows_total, 3 * D)
        .astype(jnp.bfloat16)
    )
    projected_f32 = grad_projected.astype(jnp.float32)
    grad_b_qv = jnp.concatenate(
        [jnp.sum(projected_f32[:, :D], 0), jnp.sum(projected_f32[:, 2 * D :], 0)]
    )
    grad_w_qkv = contract(input_low, grad_projected, 0, 0)
    grad_input = contract(grad_projected, w_qkv, 1, 1)
    grad_gain_attn = jnp.sum(grad_input * normed_one, 0)
    caption_grad = (
        grad_after + norm_back(grad_input * gain_attn.astype(jnp.float32), normed_one, inverse_one)
    ).reshape(local_pairs, CAP, D)
    halves = (
        lax.psum_scatter(grad_gain_attn, "rep", scatter_dimension=0, tiled=True),
        lax.psum_scatter(grad_w_qkv, "rep", scatter_dimension=1, tiled=True),
        lax.psum_scatter(grad_b_qv, "rep", scatter_dimension=0, tiled=True),
        lax.psum_scatter(grad_w_out, "rep", scatter_dimension=1, tiled=True),
        lax.psum_scatter(grad_gain_mlp, "rep", scatter_dimension=0, tiled=True),
        lax.psum_scatter(grad_w_up, "rep", scatter_dimension=1, tiled=True),
        lax.psum_scatter(grad_b_up, "rep", scatter_dimension=0, tiled=True),
        lax.psum_scatter(grad_w_down, "rep", scatter_dimension=1, tiled=True),
    )
    half_gain_a, half_qkv, half_bqv, half_out, half_gain_m, half_up, half_bup, half_down = halves
    summed = lax.psum(
        (half_gain_a, half_qkv, half_bqv, half_out, half_gain_m, half_up, half_bup, half_down), "dp"
    )
    return (
        pair_loss,
        caption_grad,
        summed[0],
        summed[1],
        summed[2],
        summed[3],
        summed[4],
        summed[5],
        summed[6],
        summed[7],
    )


def solution(mesh):
    in_specs = (
        P(("dp", "rep"), None, None),
        P(("dp", "rep")),
        P(("dp", "rep"), None, None),
        P(("dp", "rep")),
        P("rep"),
        P("rep", None),
        P("rep"),
        P("rep", None),
        P("rep"),
        P("rep", None),
        P("rep"),
        P("rep", None),
        P(),
        P(),
        P(),
        P(),
        P(),
        P(),
        P(),
        P(),
        P(),
    )
    out_specs = (
        P(("dp", "rep")),
        P(("dp", "rep"), None, None),
        P("rep"),
        P(None, "rep"),
        P("rep"),
        P(None, "rep"),
        P("rep"),
        P(None, "rep"),
        P("rep"),
        P(None, "rep"),
    )
    return jax.shard_map(local, mesh=mesh, in_specs=in_specs, out_specs=out_specs, check_vma=False)
```

profile of v0, /device:TPU:8, one launch (start us, length us, event | category | flops | bytes accessed | tf_op | source)
XLA Modules:
  0.0 1714.4 jit_solution(6546438218508723212)
XLA Ops:
  59.3 19.5 %fusion.151 = (bf16[512,3072]{1,0:T(8,128)(2,1)S(1)}, f32[512,3072]{1,0:T(8,128)}) fusion(f32[3072]{0:T(1024)S(1)} %copy-done.50, bf16[768,3072]{1,0:T(8,128)(2,1)} %param.42, f32[512,768]{1,0:T(8,128)S(1)} %get-tuple-element.310, f32[768]{0:T(1024)S(1)} %copy-done.32, f32[512]{0:T(512)S(1)} %add_rsqrt_fusion.7, f32[512]{0:T(512)S(1)} %broadcast_multiply_fusion.9), kind=kOutput, calls=%fused_computation.211 | convolution fusion | flops 2521300992 | bytes 15748096 | tf_op jit(solution)/shard_map/dot_general | solution.py:90
  100.6 19.5 %gather_fusion.1 = bf16[32,145,768]{2,0,1:T(8,128)(2,1)} fusion(bf16[32,145,768]{2,0,1:T(8,128)(2,1)} %param.25, s32[1024]{0:T(1024)} %copy-done.56), kind=kCustom, calls=%fused_computation.1 | custom fusion | bytes 14254208 | tf_op jit(solution)/shard_map/gather | solution.py:174
  130.8 700.5 %while.10 = (s32[]{:T(128)}, bf16[8,4,768]{2,1,0:T(4,128)(2,1)}, s32[8,4]{1,0:T(8,128)}, bf16[8,4,145,768]{3,2,1,0:T(8,128)(2,1)}, bf16[768]{0:T(1024)(128)(2,1)...) while((s32[]{:T(128)}, bf16[8,4,768]{2,1,0:T(4,128)(2,1)}, ...), condition=%wide.region_29.30_spmd, body=%wide.region_9.29_spmd.sunk | while | flops 8605748224 | bytes 80400800 | solution.py:184
  132.9 68.3 %conditional.7 = (bf16[1,4,768]{2,1,0:T(4,128)(2,1)}) conditional(s32[]{:T(128)} %convert_element_type.473, (bf16[8,4,145,768]{3,2,1,0:T(8,128)(2,1)}, s32[]{:T(128)}, bf16[768]{0:T(1024)(128)(2,1)}, bf16[768,2304]{1,0:T(8,128)(2,1)}, bf16[1536]{0:T(1024)(128)(2,1)S(1)}, /*index=5*/s32[1,4]{1,0:T(1,128)S(1)}, bf16[768,768]{1,0:T(8,128)(2,1)}, ...), branch_computations={%region_11.19_spmd, %region_20.28_spmd} | conditional | flops 8605748224 | bytes 80387720
  176.4 11.8 fusion.18
  204.5 60.5 %conditional.7 = (bf16[1,4,768]{2,1,0:T(4,128)(2,1)}) conditional(s32[]{:T(128)} %convert_element_type.473, (bf16[8,4,145,768]{3,2,1,0:T(8,128)(2,1)}, s32[]{:T(128)}, bf16[768]{0:T(1024)(128)(2,1)}, bf16[768,2304]{1,0:T(8,128)(2,1)}, bf16[1536]{0:T(1024)(128)(2,1)S(1)}, /*index=5*/s32[1,4]{1,0:T(1,128)S(1)}, bf16[768,768]{1,0:T(8,128)(2,1)}, ...), branch_computations={%region_11.19_spmd, %region_20.28_spmd} | conditional | flops 8605748224 | bytes 80387720
  247.9 11.8 fusion.18
  268.3 60.5 %conditional.7 = (bf16[1,4,768]{2,1,0:T(4,128)(2,1)}) conditional(s32[]{:T(128)} %convert_element_type.473, (bf16[8,4,145,768]{3,2,1,0:T(8,128)(2,1)}, s32[]{:T(128)}, bf16[768]{0:T(1024)(128)(2,1)}, bf16[768,2304]{1,0:T(8,128)(2,1)}, bf16[1536]{0:T(1024)(128)(2,1)S(1)}, /*index=5*/s32[1,4]{1,0:T(1,128)S(1)}, bf16[768,768]{1,0:T(8,128)(2,1)}, ...), branch_computations={%region_11.19_spmd, %region_20.28_spmd} | conditional | flops 8605748224 | bytes 80387720
  332.1 60.5 %conditional.7 = (bf16[1,4,768]{2,1,0:T(4,128)(2,1)}) conditional(s32[]{:T(128)} %convert_element_type.473, (bf16[8,4,145,768]{3,2,1,0:T(8,128)(2,1)}, s32[]{:T(128)}, bf16[768]{0:T(1024)(128)(2,1)}, bf16[768,2304]{1,0:T(8,128)(2,1)}, bf16[1536]{0:T(1024)(128)(2,1)S(1)}, /*index=5*/s32[1,4]{1,0:T(1,128)S(1)}, bf16[768,768]{1,0:T(8,128)(2,1)}, ...), branch_computations={%region_11.19_spmd, %region_20.28_spmd} | conditional | flops 8605748224 | bytes 80387720
  375.4 11.8 fusion.18
  395.8 60.5 %conditional.7 = (bf16[1,4,768]{2,1,0:T(4,128)(2,1)}) conditional(s32[]{:T(128)} %convert_element_type.473, (bf16[8,4,145,768]{3,2,1,0:T(8,128)(2,1)}, s32[]{:T(128)}, bf16[768]{0:T(1024)(128)(2,1)}, bf16[768,2304]{1,0:T(8,128)(2,1)}, bf16[1536]{0:T(1024)(128)(2,1)S(1)}, /*index=5*/s32[1,4]{1,0:T(1,128)S(1)}, bf16[768,768]{1,0:T(8,128)(2,1)}, ...), branch_computations={%region_11.19_spmd, %region_20.28_spmd} | conditional | flops 8605748224 | bytes 80387720
  439.2 11.8 fusion.18
  459.6 110.3 %conditional.7 = (bf16[1,4,768]{2,1,0:T(4,128)(2,1)}) conditional(s32[]{:T(128)} %convert_element_type.473, (bf16[8,4,145,768]{3,2,1,0:T(8,128)(2,1)}, s32[]{:T(128)}, bf16[768]{0:T(1024)(128)(2,1)}, bf16[768,2304]{1,0:T(8,128)(2,1)}, bf16[1536]{0:T(1024)(128)(2,1)S(1)}, /*index=5*/s32[1,4]{1,0:T(1,128)S(1)}, bf16[768,768]{1,0:T(8,128)(2,1)}, ...), branch_computations={%region_11.19_spmd, %region_20.28_spmd} | conditional | flops 8605748224 | bytes 80387720
  536.8 26.1 %fusion.100 = f32[580,768]{1,0:T(8,128)} fusion(f32[580,768]{1,0:T(8,128)} %copy-done.2, bf16[3072,768]{1,0:T(8,128)(2,1)} %get-tuple-element.174, bf16[768,3072]{1,0:T(8,128)(2,1)} %get-tuple-element.172, f32[3072]{0:T(1024)} %convert_element_type.246, f32[768]{0:T(1024)} %convert_element_type.244, f32[580]{0:T(1024)} %add_rsqrt_fusion.3, f32[580]{0:T(1024)} %copy-done.27), kind=kOutput, calls=%fused_computation.146 | convolution fusion | flops 5593390080 | bytes 13020704 | tf_op jit(solution)/shard_map/while/body/eval_jaxpr/cond/branch_1_fun/dot_general | solution.py:94
  581.3 111.6 %conditional.7 = (bf16[1,4,768]{2,1,0:T(4,128)(2,1)}) conditional(s32[]{:T(128)} %convert_element_type.473, (bf16[8,4,145,768]{3,2,1,0:T(8,128)(2,1)}, s32[]{:T(128)}, bf16[768]{0:T(1024)(128)(2,1)}, bf16[768,2304]{1,0:T(8,128)(2,1)}, bf16[1536]{0:T(1024)(128)(2,1)S(1)}, /*index=5*/s32[1,4]{1,0:T(1,128)S(1)}, bf16[768,768]{1,0:T(8,128)(2,1)}, ...), branch_computations={%region_11.19_spmd, %region_20.28_spmd} | conditional | flops 8605748224 | bytes 80387720
  659.5 26.2 %fusion.100 = f32[580,768]{1,0:T(8,128)} fusion(f32[580,768]{1,0:T(8,128)} %copy-done.2, bf16[3072,768]{1,0:T(8,128)(2,1)} %get-tuple-element.174, bf16[768,3072]{1,0:T(8,128)(2,1)} %get-tuple-element.172, f32[3072]{0:T(1024)} %convert_element_type.246, f32[768]{0:T(1024)} %convert_element_type.244, f32[580]{0:T(1024)} %add_rsqrt_fusion.3, f32[580]{0:T(1024)} %copy-done.27), kind=kOutput, calls=%fused_computation.146 | convolution fusion | flops 5593390080 | bytes 13020704 | tf_op jit(solution)/shard_map/while/body/eval_jaxpr/cond/branch_1_fun/dot_general | solution.py:94
  704.0 111.4 %conditional.7 = (bf16[1,4,768]{2,1,0:T(4,128)(2,1)}) conditional(s32[]{:T(128)} %convert_element_type.473, (bf16[8,4,145,768]{3,2,1,0:T(8,128)(2,1)}, s32[]{:T(128)}, bf16[768]{0:T(1024)(128)(2,1)}, bf16[768,2304]{1,0:T(8,128)(2,1)}, bf16[1536]{0:T(1024)(128)(2,1)S(1)}, /*index=5*/s32[1,4]{1,0:T(1,128)S(1)}, bf16[768,768]{1,0:T(8,128)(2,1)}, ...), branch_computations={%region_11.19_spmd, %region_20.28_spmd} | conditional | flops 8605748224 | bytes 80387720
  782.3 26.1 %fusion.100 = f32[580,768]{1,0:T(8,128)} fusion(f32[580,768]{1,0:T(8,128)} %copy-done.2, bf16[3072,768]{1,0:T(8,128)(2,1)} %get-tuple-element.174, bf16[768,3072]{1,0:T(8,128)(2,1)} %get-tuple-element.172, f32[3072]{0:T(1024)} %convert_element_type.246, f32[768]{0:T(1024)} %convert_element_type.244, f32[580]{0:T(1024)} %add_rsqrt_fusion.3, f32[580]{0:T(1024)} %copy-done.27), kind=kOutput, calls=%fused_computation.146 | convolution fusion | flops 5593390080 | bytes 13020704 | tf_op jit(solution)/shard_map/while/body/eval_jaxpr/cond/branch_1_fun/dot_general | solution.py:94
  837.9 225.3 %all-gather.22.cloned.1.call-done = bf16[1024,768]{1,0:T(8,128)(2,1)} async-done(((bf16[32,768]{1,0:T(8,128)(2,1)}), bf16[1024,768]{1,0:T(8,128)(2,1)}) %all-gather.22.cloned.1.call-update) | async-done | bytes 1572880 | tf_op jit(solution)/shard_map/all_gather | solution.py:213
  1072.2 100.7 %reduce-scatter.6.cloned.1.call-done = f32[32,768]{1,0:T(8,128)} async-done(((f32[1024,768]{1,0:T(8,128)}), f32[32,768]{1,0:T(8,128)}) %reduce-scatter.6.cloned.1.call-update) | async-done | bytes 98320 | tf_op jit(solution)/shard_map/reduce_scatter | solution.py:227
  1253.7 16.9 reduce-scatter.12.cloned.1.call-done
  1270.6 21.4 %reduce-scatter.14.cloned.1.call-done = f32[3072,384]{1,0:T(8,128)} async-done(((f32[3072,768]{1,0:T(8,128)}), f32[3072,384]{1,0:T(8,128)}) %reduce-scatter.14.cloned.1.call-update) | async-done | bytes 4718608 | tf_op jit(solution)/shard_map/reduce_scatter | solution.py:303
  1313.7 74.1 %all-reduce.4 = (f32[384]{0:T(512)}, f32[768]{0:T(1024)}, f32[384]{0:T(512)}, f32[1536]{0:T(1024)}) all-reduce(f32[384]{0:T(512)} %dynamic-slice.1, f32[768]{0:T(1024)} %dynamic-slice.3, f32[384]{0:T(512)} %dynamic-slice.5, f32[1536]{0:T(1024)S(1)} %dynamic-slice.7), channel_id=1, replica_groups=mesh['dp'=16,'rep'=2] {'dp'}, use_global_device_ids=true, to_apply=%region_46.47 | all-reduce | flops 3072 | bytes 24576 | tf_op jit(solution)/shard_map/psum | solution.py:306
  1393.1 303.4 %all-reduce.9.cloned.1.call-done = (f32[768,1152]{1,0:T(8,128)}, f32[768,384]{1,0:T(8,128)}, f32[768,1536]{1,0:T(8,128)}, f32[3072,384]{1,0:T(8,128)}) async-done(((f32[768,1152]{1,0:T(8,128)}, f32[768,384]{1,0:T(8,128)}, f32[768,1536]{1,0:T(8,128)}, f32[3072,384]{1,0:T(8,128)}), (f32[768,1152]{1,0:T(8,128)}, f32[768,384]{1,0:T(8,128)}, f32[768,1536]{1,0:T(8,128)}, ...) | async-done | bytes 14155792 | tf_op jit(solution)/shard_map/psum | solution.py:306
  (624 shorter events, 743.3 us)
Async XLA Ops:
  7.2 18.2 %copy-start = (bf16[768,2304]{1,0:T(8,128)(2,1)S(1)}, bf16[768,2304]{1,0:T(8,128)(2,1)}, u32[]{:S(2)}) copy-start(bf16[768,2304]{1,0:T(8,128)(2,1)} %param.38) | copy-start | bytes 10616836
  7.2 123.6 %all-gather.14.cloned.1.call-start = ((), (), s32[]{:S(2)}) async-start(), calls=%async_computation.6 | async-start | bytes 1769472 | tf_op jit(solution)/shard_map/all_gather | solution.py:164
  7.9 122.8 %all-gather.12.cloned.1.call-start = ((), (), s32[]{:S(2)}) async-start(), calls=%async_computation.5 | async-start | bytes 5308416 | tf_op jit(solution)/shard_map/all_gather | solution.py:162
  8.7 122.1 %all-gather.16.cloned.1.call-start = ((), (), s32[]{:S(2)}) async-start(), calls=%async_computation.7 | async-start | bytes 7077888 | tf_op jit(solution)/shard_map/all_gather | solution.py:166
  9.4 121.4 %all-gather.18.cloned.1.call-start = ((), (), s32[]{:S(2)}) async-start(), calls=%async_computation.8 | async-start | bytes 7077888 | tf_op jit(solution)/shard_map/all_gather | solution.py:168
  10.0 825.1 %all-gather.20.cloned.1.call-start = ((), (), s32[]{:S(2)}) async-start(), calls=%async_computation.9 | async-start | bytes 1622016 | tf_op jit(solution)/shard_map/all_gather | solution.py:212
  11.4 17.4 %copy-start.28 = (f32[32,16]{1,0:T(8,128)}, f32[32,16]{1,0:T(8,128)S(1)}, u32[]{:S(2)}) copy-start(f32[32,16]{1,0:T(8,128)S(1)} %broadcast_multiply_fusion.4) | copy-start | bytes 6148
  56.1 22.7 %slice-start = ((s8[4718592]{0:T(1024)(128)(4,1)}), s8[4194304]{0:T(1024)(128)(4,1)S(1)}, s32[]{:S(2)}) async-start(s8[4718592]{0:T(1024)(128)(4,1)} %bitcast.179), calls=%async_computation.17 | async-start | bytes 8388608
  58.9 20.0 %copy-start.5 = (f32[512,768]{1,0:T(8,128)}, f32[512,768]{1,0:T(8,128)S(1)}, u32[]{:S(2)}) copy-start(f32[512,768]{1,0:T(8,128)S(1)} %get-tuple-element.310) | copy-start | bytes 4718596
  58.9 19.9 %copy-start.40 = (f32[512]{0:T(512)}, f32[512]{0:T(512)S(1)}, u32[]{:S(2)}) copy-start(f32[512]{0:T(512)S(1)} %broadcast_multiply_fusion.9) | copy-start | bytes 6148
  59.2 19.6 %copy-start.44 = (f32[512]{0:T(512)}, f32[512]{0:T(512)S(1)}, u32[]{:S(2)}) copy-start(f32[512]{0:T(512)S(1)} %add_rsqrt_fusion.7) | copy-start | bytes 6148
  59.2 19.6 %slice-start.1 = ((s8[4718592]{0:T(1024)(128)(4,1)}), s8[524288]{0:T(1024)(128)(4,1)S(1)}, s32[]{:S(2)}) async-start(s8[4718592]{0:T(1024)(128)(4,1)} %bitcast.179), calls=%async_computation.18 | async-start | bytes 1048576
  59.3 19.6 %copy-start.35 = (f32[32,16]{1,0:T(8,128)S(1)}, f32[32,16]{1,0:T(8,128)}, u32[]{:S(2)}) copy-start(f32[32,16]{1,0:T(8,128)} %get-tuple-element.306) | copy-start | bytes 6148
  83.5 979.6 %all-gather.22.cloned.1.call-start = ((), (), s32[]{:S(2)}) async-start(), calls=%async_computation.15 | async-start | bytes 1622016 | tf_op jit(solution)/shard_map/all_gather | solution.py:213
  835.0 337.9 %reduce-scatter.6.cloned.1.call-start = ((), (), s32[]{:S(2)}) async-start(), calls=%async_computation.10 | async-start | bytes 3244032 | tf_op jit(solution)/shard_map/reduce_scatter | solution.py:227
  835.0 232.6 %copy-start.61 = (s32[32]{0:T(128)}, s32[32]{0:T(128)S(1)}, u32[]{:S(2)}) copy-start(s32[32]{0:T(128)S(1)} %iota_add_fusion) | copy-start | bytes 388
  837.8 229.8 %copy-start.52 = (f32[32]{0:T(128)}, f32[32]{0:T(128)S(1)}, u32[]{:S(2)}) copy-start(f32[32]{0:T(128)S(1)} %get-tuple-element.317) | copy-start | bytes 388
  1071.5 182.2 %reduce-scatter.10.cloned.1.call-start = ((), (), s32[]{:S(2)}) async-start(), calls=%async_computation.12 | async-start | bytes 3538944 | tf_op jit(solution)/shard_map/reduce_scatter | solution.py:299
  1072.2 104.6 %copy-start.47 = (f32[512]{0:T(512)S(1)}, f32[512]{0:T(512)}, u32[]{:S(2)}) copy-start(f32[512]{0:T(512)} %reshape.520) | copy-start | bytes 6148
  1072.2 104.8 %copy-start.51 = (f32[3072]{0:T(1024)S(1)}, f32[3072]{0:T(1024)}, u32[]{:S(2)}) copy-start(f32[3072]{0:T(1024)} %convert_element_type.301) | copy-start | bytes 36868
  1192.8 60.8 %reduce-scatter.8.cloned.1.call-start = ((), (), s32[]{:S(2)}) async-start(), calls=%async_computation.11 | async-start | bytes 10616832 | tf_op jit(solution)/shard_map/reduce_scatter | solution.py:297
  1233.9 36.7 %reduce-scatter.12.cloned.1.call-start = ((), (), s32[]{:S(2)}) async-start(), calls=%async_computation.13 | async-start | bytes 14155776 | tf_op jit(solution)/shard_map/reduce_scatter | solution.py:301
  1244.6 47.5 %reduce-scatter.14.cloned.1.call-start = ((), (), s32[]{:S(2)}) async-start(), calls=%async_computation.14 | async-start | bytes 14155776 | tf_op jit(solution)/shard_map/reduce_scatter | solution.py:303
  1253.6 442.9 %all-reduce.9.cloned.1.call-start = ((), (), s32[]{:S(2)}) async-start(), calls=%async_computation.16 | async-start | bytes 28311552 | tf_op jit(solution)/shard_map/psum | solution.py:306
  (83 other events, 234.9 us)
Sparse Core Ops, SparseCore 0:
  9.6 10.6 all-gather.13
  21.8 13.8 all-gather.11
  37.2 15.6 all-gather.15
  54.3 15.6 all-gather.17
  83.6 68.2 all-gather.19
  835.1 227.9 all-gather.21
  1071.6 101.2 reduce-scatter.5
  1193.0 9.3 reduce-scatter.9
  1234.0 15.2 reduce-scatter.7
  1251.5 19.0 reduce-scatter.11
  1272.9 19.0 reduce-scatter.13
  1298.3 398.0 all-reduce.8
where the time goes:
time: 1710 us
  waiting for transfers between devices  670 us (39%)
  matrix products  381 us (22%)
  local copies, waits for them, and re-layouts  347 us (20%)
  other arithmetic  165 us (10%)
  blocking collectives  85.9 us (5%)
  loops' own time  47.3 us (3%)
  between operations  17.3 us (1%)
    psum x1, waiting for transfers between devices, local(): lax.psum((half_gain_a, half_qkv, half_bqv, half_out, half_gain_m, half_up...  303 us
    all_gather x1, waiting for transfers between devices, local(): lax.all_gather(image_emb, ('dp', 'rep'), axis=0, tiled=True)  225 us
    dot_general x9, matrix products, block_forward(): jnp.dot(hidden, weight_down, preferred_element_type=jnp.float32)  140 us
    reduce_scatter x1, waiting for transfers between devices, local(): lax.psum_scatter(contract(image_sgrad, image_emb, 0, 0) * SCALE, ('dp', '...  101 us
    psum x1, blocking collectives, local(): lax.psum((half_gain_a, half_qkv, half_bqv, half_out, half_gain_m, half_up...  74.1 us
    dot_general x13, matrix products, contract(): lax.dot_general(left_side, right_side, (((left_dim,), (right_dim,)), ((),...  59.1 us
    reshape x9, local copies, waits for them, and re-layouts, block_forward(): projected = projected.reshape(number, span_len, 3, HEADS, head_dim)  56.6 us
    another operation x76, local copies, waits for them, and re-layouts  52.4 us
  transfers between devices with their start and end apart: 12, of which 5 were waited for; matrix products, arithmetic and copies ran while one was open for 49% of the time, Pallas kernels for 0%

commit v1 on v0

--- a/solution.py
+++ b/solution.py
@@ -124,14 +124,135 @@
     )
 
 
-def half_softmax(scores, own_pair):
-    maxima = jnp.max(scores, -1, keepdims=True)
+MOST_PAIRS = 2048
+
+
+def dp_bits(size):
+    bits, bit = [], 1
+    while bit < size:
+        bits.append(bit)
+        bit *= 2
+    return bits
+
+
+def swap(values, axis, bit):
+    size = lax.axis_size(axis)
+    return lax.ppermute(values, axis, [(place, place ^ bit) for place in range(size)])
+
+
+def gather_relative(values):
+    for bit in reversed(dp_bits(lax.axis_size("dp"))):
+        values = jnp.concatenate([values, swap(values, "dp", bit)], 0)
+    return jnp.concatenate([values, swap(values, "rep", 1)], 0)
+
+
+def relative_chunks():
+    bits = dp_bits(lax.axis_size("dp"))
+    offsets = [0]
+    for bit in reversed(bits):
+        offsets = offsets + [entry + bit for entry in offsets]
+    places = sorted(range(len(offsets)), key=lambda place: place)
+    table = []
+    for place in places:
+        total, rest = 0, place
+        for level, bit in enumerate(reversed(bits)):
+            if place & (1 << level):
+                total += bit
+        table.append(total)
+    return lax.axis_index("dp") ^ jnp.array(table, jnp.int32)
+
+
+def reduce_halving(chunks):
+    for bit in dp_bits(lax.axis_size("dp")):
+        half = chunks.shape[0] // 2
+        arrived = swap(chunks[half:].astype(jnp.bfloat16), "dp", bit)
+        chunks = chunks[:half] + arrived.astype(jnp.float32)
+    return chunks
+
+
+def spread_doubling(chunks):
+    for bit in reversed(dp_bits(lax.axis_size("dp"))):
+        chunks = jnp.concatenate([chunks, swap(chunks, "dp", bit)], 0)
+    return chunks
+
+
+def sum_over_chips(own_half, order):
+    size = lax.axis_size("dp")
+    rows, columns = own_half.shape
+    chunks = own_half.reshape(size, rows // size, columns)[order]
+    done = spread_doubling(reduce_halving(chunks).astype(jnp.bfloat16))
+    return done[jnp.argsort(order)].reshape(rows, columns).astype(jnp.float32)
+
+
+def sum_over_pair(left_side, right_side):
+    half = right_side.shape[1] // 2
+    mine = lax.axis_index("rep")
+    own_side = lax.dynamic_slice_in_dim(right_side, mine * half, half, 1)
+    other_side = lax.dynamic_slice_in_dim(right_side, (1 - mine) * half, half, 1)
+    arrived = swap(contract(left_side, other_side, 0, 0).astype(jnp.bfloat16), "rep", 1)
+    return contract(left_side, own_side, 0, 0) + arrived.astype(jnp.float32)
+
+
+def softmax_parts(scores, axis):
+    maxima = jnp.max(scores, axis, keepdims=True)
     powers = jnp.exp(scores - maxima)
-    totals = jnp.sum(powers, -1, keepdims=True)
-    log_total = maxima[:, 0] + jnp.log(totals[:, 0])
-    loss_part = log_total - jnp.sum(scores * own_pair, -1)
-    grad_part = (0.5 * (powers / totals - own_pair)).astype(jnp.bfloat16)
-    return (loss_part, grad_part, log_total)
+    totals = jnp.sum(powers, axis, keepdims=True)
+    return powers / totals, maxima + jnp.log(totals)
+
+
+def text_unit(pooled_low, text_proj):
+    proj_out = jnp.dot(pooled_low, text_proj, preferred_element_type=jnp.float32)
+    inverse_z = lax.rsqrt(jnp.sum(proj_out * proj_out, -1, keepdims=True) + EPS)
+    return proj_out * inverse_z, inverse_z
+
+
+def branch_grad(grad_unit, unit_text, inverse_z, text_proj, lengths):
+    grad_projout = (
+        inverse_z * (grad_unit - unit_text * jnp.sum(unit_text * grad_unit, -1, keepdims=True))
+    ).astype(jnp.bfloat16)
+    return contract(grad_projout, text_proj, 1, 1) / lengths
+
+
+def loss_whole(pooled_all, image_all, text_proj, lengths_all, local_pairs):
+    unit_text, inverse_z = text_unit(pooled_all, text_proj)
+    total = pooled_all.shape[0]
+    scores = contract(unit_text.astype(jnp.bfloat16), image_all, 1, 1) * SCALE
+    by_text, text_total = softmax_parts(scores, 1)
+    by_image, image_total = softmax_parts(scores, 0)
+    same = (
+        jnp.arange(total, dtype=jnp.int32)[:, None] == jnp.arange(total, dtype=jnp.int32)[None, :]
+    ).astype(jnp.float32)
+    own = jnp.sum(scores[:local_pairs] * same[:local_pairs], -1)
+    pair_loss = 0.5 * (text_total[:local_pairs, 0] - own) + 0.5 * (
+        image_total[0, :local_pairs] - own
+    )
+    sgrad = (0.5 * (by_text - same) + 0.5 * (by_image - same)).astype(jnp.bfloat16)
+    grad_unit = contract(sgrad, image_all, 1, 0) * SCALE
+    grads = branch_grad(grad_unit, unit_text, inverse_z, text_proj, lengths_all)
+    return pair_loss, grads[:local_pairs], grads.astype(jnp.bfloat16)
+
+
+def loss_rows(pooled_all, image_all, text_proj, lengths_all, local_pairs):
+    unit_all, inverse_all = text_unit(pooled_all, text_proj)
+    unit_text, inverse_z = unit_all[:local_pairs], inverse_all[:local_pairs]
+    text_all = unit_all.astype(jnp.bfloat16)
+    total = pooled_all.shape[0]
+    text_scores = contract(text_all[:local_pairs], image_all, 1, 1) * SCALE
+    image_scores = contract(image_all[:local_pairs], text_all, 1, 1) * SCALE
+    by_text, text_total = softmax_parts(text_scores, 1)
+    image_total = softmax_parts(image_scores, 1)[1]
+    every_total = gather_relative(image_total)
+    same = (
+        jnp.arange(local_pairs, dtype=jnp.int32)[:, None]
+        == jnp.arange(total, dtype=jnp.int32)[None, :]
+    ).astype(jnp.float32)
+    own = jnp.sum(text_scores * same, -1)
+    pair_loss = 0.5 * (text_total[:, 0] - own) + 0.5 * (image_total[:, 0] - own)
+    by_image = jnp.exp(text_scores - every_total[:, 0][None, :])
+    sgrad = (0.5 * (by_text - same) + 0.5 * (by_image - same)).astype(jnp.bfloat16)
+    grad_unit = contract(sgrad, image_all, 1, 0) * SCALE
+    grads = branch_grad(grad_unit, unit_text, inverse_z, text_proj, lengths_all[:local_pairs])
+    return pair_loss, grads, grads.astype(jnp.bfloat16)
 
 
 def local(
@@ -181,10 +302,6 @@
             lambda: image_embed(pixels[:, :LOWLEN], length, frozen),
         )
 
-    sorted_emb = lax.map(image_block, (stacked, sorted_len.reshape(blocks, IMG_BLK))).reshape(
-        local_pairs, D
-    )
-    image_emb = sorted_emb[jnp.argsort(ordering)]
     params = (gain_attn, w_qkv, b_qv, w_out, gain_mlp, w_up, b_up, w_down)
     pooled, saved = block_forward(captions, cap_lengths, params)
     (
@@ -204,55 +321,54 @@
         hidden,
         valid_key,
     ) = saved
-    proj_out = jnp.dot(pooled.astype(jnp.bfloat16), text_proj, preferred_element_type=jnp.float32)
-    inverse_z = lax.rsqrt(jnp.sum(proj_out * proj_out, -1, keepdims=True) + EPS)
-    unit_text = proj_out * inverse_z
-    text_emb = unit_text.astype(jnp.bfloat16)
-    all_text, all_image = (
-        lax.all_gather(text_emb, ("dp", "rep"), axis=0, tiled=True),
-        lax.all_gather(image_emb, ("dp", "rep"), axis=0, tiled=True),
-    )
-    total_pairs = all_text.shape[0]
-    first_row = lax.axis_index(("dp", "rep")) * local_pairs
-    own_pair = (
-        jnp.arange(total_pairs, dtype=jnp.int32)[None, :]
-        == first_row + jnp.arange(local_pairs, dtype=jnp.int32)[:, None]
-    ).astype(jnp.float32)
-    text_scores = contract(text_emb, all_image, 1, 1) * SCALE
-    image_scores = contract(image_emb, all_text, 1, 1) * SCALE
-    text_loss, text_sgrad, text_total = half_softmax(text_scores, own_pair)
-    image_loss, image_sgrad, image_total = half_softmax(image_scores, own_pair)
-    pair_loss = 0.5 * text_loss + 0.5 * image_loss
-    row_part = contract(text_sgrad, all_image, 1, 0) * SCALE
-    column_part = lax.psum_scatter(
-        contract(image_sgrad, image_emb, 0, 0) * SCALE,
-        ("dp", "rep"),
-        scatter_dimension=0,
-        tiled=True,
-    )
-    grad_unit = row_part + column_part
-    grad_projout = (
-        inverse_z * (grad_unit - unit_text * jnp.sum(unit_text * grad_unit, -1, keepdims=True))
+    valid_rows = valid_key.astype(jnp.float32)[:, :, None]
+    hidden_sum = jnp.sum(
+        hidden.astype(jnp.float32).reshape(local_pairs, CAP, -1) * valid_rows, 1
     ).astype(jnp.bfloat16)
-    grad_pooled = contract(grad_projout, text_proj, 1, 1)
+    slope = gelu_slope(pre_act).reshape(local_pairs, CAP, -1) * valid_rows
+    lengths = cap_lengths.astype(jnp.float32)[:, None]
+    total_pairs = local_pairs * lax.axis_size("dp") * lax.axis_size("rep")
+    whole = total_pairs <= MOST_PAIRS
+    sent = [
+        pooled.astype(jnp.bfloat16),
+        jnp.broadcast_to(lengths, (local_pairs, 128)).astype(jnp.bfloat16),
+    ]
+    early = gather_relative(jnp.concatenate(sent + [hidden_sum] if whole else sent, 1))
+    sorted_emb = lax.map(image_block, (stacked, sorted_len.reshape(blocks, IMG_BLK))).reshape(
+        local_pairs, D
+    )
+    image_emb = sorted_emb[jnp.argsort(ordering)]
+    image_all = gather_relative(image_emb)
+    pooled_all = early[:, :D]
+    lengths_all = early[:, D : D + 1].astype(jnp.float32)
+    loss_of = loss_whole if whole else loss_rows
+    pair_loss, grad_pooled, branch_all = loss_of(
+        pooled_all, image_all, text_proj, lengths_all, local_pairs
+    )
+    order = relative_chunks()
+    if whole:
+        half_dim = D // 2
+        grad_w_down = contract(
+            early[:, D + 128 :],
+            lax.dynamic_slice_in_dim(branch_all, lax.axis_index("rep") * half_dim, half_dim, 1),
+            0,
+            0,
+        )
+    else:
+        grad_w_down = sum_over_chips(sum_over_pair(hidden_sum, branch_all), order)
     rows_total = local_pairs * CAP
-    grad_rows = (
-        (grad_pooled / cap_lengths.astype(jnp.float32)[:, None])[:, None, :]
-        * valid_key.astype(jnp.float32)[:, :, None]
-    ).reshape(rows_total, D)
-    grad_branch = grad_rows.astype(jnp.bfloat16)
-    grad_w_down = contract(hidden, grad_branch, 0, 0)
-    grad_hidden = contract(grad_branch, w_down, 1, 1)
-    grad_pre = (grad_hidden * gelu_slope(pre_act)).astype(jnp.bfloat16)
+    grad_rows = (grad_pooled[:, None, :] * valid_rows).reshape(rows_total, D)
+    grad_hidden = contract(branch_all[:local_pairs], w_down, 1, 1)
+    grad_pre = (grad_hidden[:, None, :] * slope).astype(jnp.bfloat16).reshape(rows_total, -1)
     grad_b_up = jnp.sum(grad_pre.astype(jnp.float32), 0)
-    grad_w_up = contract(mlp_in, grad_pre, 0, 0)
+    grad_w_up = sum_over_chips(sum_over_pair(mlp_in, grad_pre), order)
     grad_mlp_in = contract(grad_pre, w_up, 1, 1)
     grad_gain_mlp = jnp.sum(grad_mlp_in * normed_two, 0)
     grad_after = grad_rows + norm_back(
         grad_mlp_in * gain_mlp.astype(jnp.float32), normed_two, inverse_two
     )
     grad_out_low = grad_after.astype(jnp.bfloat16)
-    grad_w_out = contract(mixed_heads, grad_out_low, 0, 0)
+    grad_w_out = sum_over_chips(sum_over_pair(mixed_heads, grad_out_low), order)
     head_dim = D // HEADS
     scale_q = 1.0 / math.sqrt(head_dim)
     grad_mixed = (
@@ -286,37 +402,31 @@
     grad_b_qv = jnp.concatenate(
         [jnp.sum(projected_f32[:, :D], 0), jnp.sum(projected_f32[:, 2 * D :], 0)]
     )
-    grad_w_qkv = contract(input_low, grad_projected, 0, 0)
+    grad_w_qkv = sum_over_chips(sum_over_pair(input_low, grad_projected), order)
     grad_input = contract(grad_projected, w_qkv, 1, 1)
     grad_gain_attn = jnp.sum(grad_input * normed_one, 0)
     caption_grad = (
         grad_after + norm_back(grad_input * gain_attn.astype(jnp.float32), normed_one, inverse_one)
     ).reshape(local_pairs, CAP, D)
-    halves = (
-        lax.psum_scatter(grad_gain_attn, "rep", scatter_dimension=0, tiled=True),
-        lax.psum_scatter(grad_w_qkv, "rep", scatter_dimension=1, tiled=True),
-        lax.psum_scatter(grad_b_qv, "rep", scatter_dimension=0, tiled=True),
-        lax.psum_scatter(grad_w_out, "rep", scatter_dimension=1, tiled=True),
-        lax.psum_scatter(grad_gain_mlp, "rep", scatter_dimension=0, tiled=True),
-        lax.psum_scatter(grad_w_up, "rep", scatter_dimension=1, tiled=True),
-        lax.psum_scatter(grad_b_up, "rep", scatter_dimension=0, tiled=True),
-        lax.psum_scatter(grad_w_down, "rep", scatter_dimension=1, tiled=True),
-    )
-    half_gain_a, half_qkv, half_bqv, half_out, half_gain_m, half_up, half_bup, half_down = halves
-    summed = lax.psum(
-        (half_gain_a, half_qkv, half_bqv, half_out, half_gain_m, half_up, half_bup, half_down), "dp"
-    )
+    small = (grad_gain_attn, grad_b_qv, grad_gain_mlp, grad_b_up)
+    packed = jnp.concatenate([entry.reshape(2, -1) for entry in small], 1)
+    packed = lax.psum(packed, ("dp", "rep"))[lax.axis_index("rep")]
+    summed, start = [], 0
+    for entry in small:
+        size = entry.shape[0] // 2
+        summed.append(packed[start : start + size])
+        start += size
     return (
         pair_loss,
         caption_grad,
         summed[0],
+        grad_w_qkv,
         summed[1],
+        grad_w_out,
         summed[2],
+        grad_w_up,
         summed[3],
-        summed[4],
-        summed[5],
-        summed[6],
-        summed[7],
+        grad_w_down,
     )
 
 

time: 1710 us -> 1420 us (0.83); the launches traced: 1710 us -> 1410 us
  waiting for transfers between devices: 670 us -> 130 us
  starting transfers between devices: 0.74 us -> 108 us
  local copies, waits for them, and re-layouts: 347 us -> 434 us
  other arithmetic: 165 us -> 202 us
  blocking collectives: 85.9 us -> 54.6 us
  loops' own time: 47.3 us -> 64.8 us
    psum x1 -> x0, waiting for transfers between devices: 303 us -> none  [local(): lax.psum((half_gain_a, half_qkv, half_bqv, half_out, half_gain_m, half_up...]
    all_gather x2 -> x0, waiting for transfers between devices: 225 us -> none  [the longest x1 225 us: local(): lax.all_gather(image_emb, ('dp', 'rep'), axis=0, tiled=True)]
    reduce_scatter x5 -> x0, waiting for transfers between devices: 139 us -> none  [the longest x1 101 us: local(): lax.psum_scatter(contract(image_sgrad, image_emb, 0, 0) * SCALE, ('dp', '...]
    ppermute x0 -> x37, waiting for transfers between devices: none -> 128 us  [swap(): lax.ppermute(values, axis, [(place, place ^ bit) for place in range(size)])]
    ppermute x0 -> x37, starting transfers between devices: none -> 108 us  [swap(): lax.ppermute(values, axis, [(place, place ^ bit) for place in range(size)])]
    psum x1, blocking collectives: 74.1 us -> 47.5 us  [local(): packed = lax.psum(packed, ('dp', 'rep'))[lax.axis_index('rep')]]
    gather x0 -> x6, local copies, waits for them, and re-layouts: none -> 23.3 us  [the longest x3 13.2 us: sum_over_chips(): chunks = own_half.reshape(size, rows // size, columns)[order]]
    another operation x1, loops' own time: 35.9 us -> 53.8 us  [local(): lax.map(image_block, (stacked, sorted_len.reshape(blocks, IMG_BLK)))]
  transfers between devices with their start and end apart: 12 -> 41, of which waited for: 5 -> 21; matrix products, arithmetic and copies ran while one was open for 49% -> 66% of each run, Pallas kernels for 0% -> 0%
where the time goes in v1:
time: 1420 us; the launch traced here: 1410 us
  local copies, waits for them, and re-layouts  434 us (31%)
  matrix products  397 us (28%)
  other arithmetic  202 us (14%)
  waiting for transfers between devices  130 us (9%)
  starting transfers between devices  108 us (8%)
  loops' own time  64.8 us (5%)
  blocking collectives  54.6 us (4%)
  between operations  15.1 us (1%)
    dot_general x9, matrix products, block_forward(): jnp.dot(hidden, weight_down, preferred_element_type=jnp.float32)  155 us
    ppermute x37, waiting for transfers between devices, swap(): lax.ppermute(values, axis, [(place, place ^ bit) for place in range(size)])  128 us
    ppermute x37, starting transfers between devices, swap(): lax.ppermute(values, axis, [(place, place ^ bit) for place in range(size)])  108 us
    reshape x9, local copies, waits for them, and re-layouts, block_forward(): projected = projected.reshape(number, span_len, 3, HEADS, head_dim)  62.3 us
    another operation x109, local copies, waits for them, and re-layouts  58.8 us
    another operation x1, loops' own time, local(): lax.map(image_block, (stacked, sorted_len.reshape(blocks, IMG_BLK)))  53.8 us
    dot_general x14, matrix products, contract(): lax.dot_general(left_side, right_side, (((left_dim,), (right_dim,)), ((),...  50 us
    psum x1, blocking collectives, local(): packed = lax.psum(packed, ('dp', 'rep'))[lax.axis_index('rep')]  47.5 us
  transfers between devices with their start and end apart: 41, of which 21 were waited for; matrix products, arithmetic and copies ran while one was open for 66% of the time, Pallas kernels for 0%

profile of v1, /device:TPU:8, one launch (start us, length us, event | category | flops | bytes accessed | tf_op | source)
XLA Modules:
  0.0 1406.4 jit_solution(1978487388458586878)
XLA Ops:
  58.0 21.2 %fusion.161 = (bf16[32,3072]{1,0:T(8,128)(2,1)S(1)}, bf16[512,3072]{1,0:T(8,128)(2,1)S(1)}, f32[512,3072]{1,0:T(8,128)}) fusion(f32[32,16]{1,0:T(8,128)S(1)} %get-tuple-element.333, f32[3072]{0:T(1024)S(1)} %copy-done.59, bf16[768,3072]{1,0:T(8,128)(2,1)} %param.43, f32[512,768]{1,0:T(8,128)S(1)} %get-tuple-element.337, ...), kind=kOutput, calls=%fused_computation.227 | convolution fusion | flops 2525921280 | bytes 15946752 | tf_op jit(solution)/shard_map/dot_general | solution.py:90
  98.6 12.5 collective-permute-done.1
  120.5 16.6 %collective-permute-done.2 = bf16[128,3968]{1,0:T(8,128)(2,1)} collective-permute-done((bf16[128,3968]{1,0:T(8,128)(2,1)}, bf16[128,3968]{1,0:T(8,128)(2,1)}, u32[]{:S(2)}, u32[]{:S(2)}) %collective-permute-start.2) | collective-permute-done | bytes 1015840 | tf_op jit(solution)/shard_map/ppermute | solution.py:140
  143.2 19.3 %gather_fusion.1 = bf16[32,145,768]{2,0,1:T(8,128)(2,1)} fusion(bf16[32,145,768]{2,0,1:T(8,128)(2,1)} %param.26, s32[1024]{0:T(1024)S(1)} %pad_clamp_fusion.3), kind=kCustom, calls=%fused_computation.1 | custom fusion | bytes 14254208 | tf_op jit(solution)/shard_map/gather | solution.py:295
  195.4 754.0 %while.10 = (s32[]{:T(128)}, bf16[8,4,768]{2,1,0:T(4,128)(2,1)}, s32[8,4]{1,0:T(8,128)}, bf16[8,4,145,768]{3,2,1,0:T(8,128)(2,1)}, bf16[768]{0:T(1024)(128)(2,1)...) while((s32[]{:T(128)}, bf16[8,4,768]{2,1,0:T(4,128)(2,1)}, ...), condition=%wide.region_30.31_spmd, body=%wide.region_10.30_spmd.sunk | while | flops 8605748224 | bytes 80409320 | solution.py:337
  198.3 66.7 %conditional.7 = (bf16[1,4,768]{2,1,0:T(4,128)(2,1)}) conditional(s32[]{:T(128)} %convert_element_type.604, (bf16[8,4,145,768]{3,2,1,0:T(8,128)(2,1)}, s32[]{:T(128)}, bf16[768]{0:T(1024)(128)(2,1)}, bf16[768,2304]{1,0:T(8,128)(2,1)}, bf16[1536]{0:T(1024)(128)(2,1)S(1)}, /*index=5*/s32[1,4]{1,0:T(1,128)}, bf16[768,768]{1,0:T(8,128)(2,1)}, ...), branch_computations={%region_12.20_spmd, %region_21.29_spmd} | conditional | flops 8605748224 | bytes 80396240
  240.7 11.8 fusion.18
  276.8 59.0 %conditional.7 = (bf16[1,4,768]{2,1,0:T(4,128)(2,1)}) conditional(s32[]{:T(128)} %convert_element_type.604, (bf16[8,4,145,768]{3,2,1,0:T(8,128)(2,1)}, s32[]{:T(128)}, bf16[768]{0:T(1024)(128)(2,1)}, bf16[768,2304]{1,0:T(8,128)(2,1)}, bf16[1536]{0:T(1024)(128)(2,1)S(1)}, /*index=5*/s32[1,4]{1,0:T(1,128)}, bf16[768,768]{1,0:T(8,128)(2,1)}, ...), branch_computations={%region_12.20_spmd, %region_21.29_spmd} | conditional | flops 8605748224 | bytes 80396240
  319.1 11.8 fusion.18
  339.6 59.0 %conditional.7 = (bf16[1,4,768]{2,1,0:T(4,128)(2,1)}) conditional(s32[]{:T(128)} %convert_element_type.604, (bf16[8,4,145,768]{3,2,1,0:T(8,128)(2,1)}, s32[]{:T(128)}, bf16[768]{0:T(1024)(128)(2,1)}, bf16[768,2304]{1,0:T(8,128)(2,1)}, bf16[1536]{0:T(1024)(128)(2,1)S(1)}, /*index=5*/s32[1,4]{1,0:T(1,128)}, bf16[768,768]{1,0:T(8,128)(2,1)}, ...), branch_computations={%region_12.20_spmd, %region_21.29_spmd} | conditional | flops 8605748224 | bytes 80396240
  381.9 11.8 fusion.18
  402.4 59.0 %conditional.7 = (bf16[1,4,768]{2,1,0:T(4,128)(2,1)}) conditional(s32[]{:T(128)} %convert_element_type.604, (bf16[8,4,145,768]{3,2,1,0:T(8,128)(2,1)}, s32[]{:T(128)}, bf16[768]{0:T(1024)(128)(2,1)}, bf16[768,2304]{1,0:T(8,128)(2,1)}, bf16[1536]{0:T(1024)(128)(2,1)S(1)}, /*index=5*/s32[1,4]{1,0:T(1,128)}, bf16[768,768]{1,0:T(8,128)(2,1)}, ...), branch_computations={%region_12.20_spmd, %region_21.29_spmd} | conditional | flops 8605748224 | bytes 80396240
  444.8 11.8 fusion.18
  465.2 107.6 %conditional.7 = (bf16[1,4,768]{2,1,0:T(4,128)(2,1)}) conditional(s32[]{:T(128)} %convert_element_type.604, (bf16[8,4,145,768]{3,2,1,0:T(8,128)(2,1)}, s32[]{:T(128)}, bf16[768]{0:T(1024)(128)(2,1)}, bf16[768,2304]{1,0:T(8,128)(2,1)}, bf16[1536]{0:T(1024)(128)(2,1)S(1)}, /*index=5*/s32[1,4]{1,0:T(1,128)}, bf16[768,768]{1,0:T(8,128)(2,1)}, ...), branch_computations={%region_12.20_spmd, %region_21.29_spmd} | conditional | flops 8605748224 | bytes 80396240
  539.8 26.3 %fusion.100 = f32[580,768]{1,0:T(8,128)} fusion(f32[580,768]{1,0:T(8,128)} %copy-done.2, bf16[3072,768]{1,0:T(8,128)(2,1)} %get-tuple-element.174, bf16[768,3072]{1,0:T(8,128)(2,1)} %get-tuple-element.172, f32[3072]{0:T(1024)} %convert_element_type.308, f32[768]{0:T(1024)} %convert_element_type.306, f32[580]{0:T(1024)} %add_rsqrt_fusion.3, ...), kind=kOutput, calls=%fused_computation.152 | convolution fusion | flops 5593390080 | bytes 13020704 | tf_op jit(solution)/shard_map/while/body/eval_jaxpr/cond/branch_1_fun/dot_general | solution.py:94
  584.5 107.8 %conditional.7 = (bf16[1,4,768]{2,1,0:T(4,128)(2,1)}) conditional(s32[]{:T(128)} %convert_element_type.604, (bf16[8,4,145,768]{3,2,1,0:T(8,128)(2,1)}, s32[]{:T(128)}, bf16[768]{0:T(1024)(128)(2,1)}, bf16[768,2304]{1,0:T(8,128)(2,1)}, bf16[1536]{0:T(1024)(128)(2,1)S(1)}, /*index=5*/s32[1,4]{1,0:T(1,128)}, bf16[768,768]{1,0:T(8,128)(2,1)}, ...), branch_computations={%region_12.20_spmd, %region_21.29_spmd} | conditional | flops 8605748224 | bytes 80396240
  659.6 26.2 %fusion.100 = f32[580,768]{1,0:T(8,128)} fusion(f32[580,768]{1,0:T(8,128)} %copy-done.2, bf16[3072,768]{1,0:T(8,128)(2,1)} %get-tuple-element.174, bf16[768,3072]{1,0:T(8,128)(2,1)} %get-tuple-element.172, f32[3072]{0:T(1024)} %convert_element_type.308, f32[768]{0:T(1024)} %convert_element_type.306, f32[580]{0:T(1024)} %add_rsqrt_fusion.3, ...), kind=kOutput, calls=%fused_computation.152 | convolution fusion | flops 5593390080 | bytes 13020704 | tf_op jit(solution)/shard_map/while/body/eval_jaxpr/cond/branch_1_fun/dot_general | solution.py:94
  704.2 108.0 %conditional.7 = (bf16[1,4,768]{2,1,0:T(4,128)(2,1)}) conditional(s32[]{:T(128)} %convert_element_type.604, (bf16[8,4,145,768]{3,2,1,0:T(8,128)(2,1)}, s32[]{:T(128)}, bf16[768]{0:T(1024)(128)(2,1)}, bf16[768,2304]{1,0:T(8,128)(2,1)}, bf16[1536]{0:T(1024)(128)(2,1)S(1)}, /*index=5*/s32[1,4]{1,0:T(1,128)}, bf16[768,768]{1,0:T(8,128)(2,1)}, ...), branch_computations={%region_12.20_spmd, %region_21.29_spmd} | conditional | flops 8605748224 | bytes 80396240
  779.1 26.3 %fusion.100 = f32[580,768]{1,0:T(8,128)} fusion(f32[580,768]{1,0:T(8,128)} %copy-done.2, bf16[3072,768]{1,0:T(8,128)(2,1)} %get-tuple-element.174, bf16[768,3072]{1,0:T(8,128)(2,1)} %get-tuple-element.172, f32[3072]{0:T(1024)} %convert_element_type.308, f32[768]{0:T(1024)} %convert_element_type.306, f32[580]{0:T(1024)} %add_rsqrt_fusion.3, ...), kind=kOutput, calls=%fused_computation.152 | convolution fusion | flops 5593390080 | bytes 13020704 | tf_op jit(solution)/shard_map/while/body/eval_jaxpr/cond/branch_1_fun/dot_general | solution.py:94
  823.8 107.8 %conditional.7 = (bf16[1,4,768]{2,1,0:T(4,128)(2,1)}) conditional(s32[]{:T(128)} %convert_element_type.604, (bf16[8,4,145,768]{3,2,1,0:T(8,128)(2,1)}, s32[]{:T(128)}, bf16[768]{0:T(1024)(128)(2,1)}, bf16[768,2304]{1,0:T(8,128)(2,1)}, bf16[1536]{0:T(1024)(128)(2,1)S(1)}, /*index=5*/s32[1,4]{1,0:T(1,128)}, bf16[768,768]{1,0:T(8,128)(2,1)}, ...), branch_computations={%region_12.20_spmd, %region_21.29_spmd} | conditional | flops 8605748224 | bytes 80396240
  898.9 26.2 %fusion.100 = f32[580,768]{1,0:T(8,128)} fusion(f32[580,768]{1,0:T(8,128)} %copy-done.2, bf16[3072,768]{1,0:T(8,128)(2,1)} %get-tuple-element.174, bf16[768,3072]{1,0:T(8,128)(2,1)} %get-tuple-element.172, f32[3072]{0:T(1024)} %convert_element_type.308, f32[768]{0:T(1024)} %convert_element_type.306, f32[580]{0:T(1024)} %add_rsqrt_fusion.3, ...), kind=kOutput, calls=%fused_computation.152 | convolution fusion | flops 5593390080 | bytes 13020704 | tf_op jit(solution)/shard_map/while/body/eval_jaxpr/cond/branch_1_fun/dot_general | solution.py:94
  972.8 56.8 %collective-permute-start.8 = (bf16[256,768]{1,0:T(8,128)(2,1)S(1)}, bf16[256,768]{1,0:T(8,128)(2,1)S(1)}, u32[]{:S(2)}, u32[]{:S(2)}) collective-permute-start(bf16[256,768]{1,0:T(8,128)(2,1)S(1)} %pad_maximum_fusion.10), channel_id=1, source_target_pairs={{0,2},{2,0},{4,6},{6,4},{8,10},{10,8},{12,14},{14,12},{16,18},{18,... | collective-permute-start | bytes 1179656 | tf_op jit(solution)/shard_map/ppermute | solution.py:140
  1200.2 47.5 %psum.7 = f32[2,3072]{1,0:T(2,128)} all-reduce(f32[2,3072]{1,0:T(2,128)} %pad_maximum_fusion.19), channel_id=1, replica_groups=mesh['dp'=16,'rep'=2] {'dp','rep'}, use_global_device_ids=true, to_apply=%region_48.49 | all-reduce | flops 6144 | bytes 49152 | tf_op jit(solution)/shard_map/psum | solution.py:413
  1289.9 17.0 %collective-permute-done.29 = bf16[8,48,1536]{2,1,0:T(8,128)(2,1)S(1)} collective-permute-done((bf16[8,48,1536]{2,1,0:T(8,128)(2,1)S(1)}, bf16[8,48,1536]{2,1,0:T(8,128)(2,1)S(1)}, u32[]{:S(2)}, u32[]{:S(2)}) %collective-permute-start.29) | collective-permute-done | bytes 1179680 | tf_op jit(solution)/shard_map/ppermute | solution.py:140
  (829 shorter events, 983.4 us)
Async XLA Ops:
  7.2 188.2 %all-gather.11.cloned.1.call-start = ((), (), s32[]{:S(2)}) async-start(), calls=%async_computation.1 | async-start | bytes 1769472 | tf_op jit(solution)/shard_map/all_gather | solution.py:285
  7.9 187.4 %all-gather.9.cloned.1.call-start = ((), (), s32[]{:S(2)}) async-start(), calls=%async_computation | async-start | bytes 5308416 | tf_op jit(solution)/shard_map/all_gather | solution.py:283
  8.7 186.7 %all-gather.13.cloned.1.call-start = ((), (), s32[]{:S(2)}) async-start(), calls=%async_computation.2 | async-start | bytes 7077888 | tf_op jit(solution)/shard_map/all_gather | solution.py:287
  9.4 186.0 %all-gather.15.cloned.1.call-start = ((), (), s32[]{:S(2)}) async-start(), calls=%async_computation.3 | async-start | bytes 7077888 | tf_op jit(solution)/shard_map/all_gather | solution.py:289
  97.2 13.8 collective-permute-start.1
  113.5 23.7 %collective-permute-start.2 = (bf16[128,3968]{1,0:T(8,128)(2,1)}, bf16[128,3968]{1,0:T(8,128)(2,1)}, u32[]{:S(2)}, u32[]{:S(2)}) collective-permute-start(bf16[128,3968]{1,0:T(8,128)(2,1)} %pad_maximum_fusion.5), channel_id=1, source_target_pairs={{0,4},{2,6},{4,0},{6,2},{8,12},{10,14},{12,8},{14,10},{16,20},{18,... | collective-permute-start | bytes 3047432 | tf_op jit(solution)/shard_map/ppermute | solution.py:140
  139.8 51.5 %collective-permute-start.3 = (bf16[256,3968]{1,0:T(8,128)(2,1)}, bf16[256,3968]{1,0:T(8,128)(2,1)}, u32[]{:S(2)}, u32[]{:S(2)}) collective-permute-start(bf16[256,3968]{1,0:T(8,128)(2,1)} %pad_maximum_fusion.3), channel_id=1, source_target_pairs={{0,2},{2,0},{4,6},{6,4},{8,10},{10,8},{12,14},{14,12},{16,18},{18,... | collective-permute-start | bytes 6094856 | tf_op jit(solution)/shard_map/ppermute | solution.py:140
  195.2 852.8 %collective-permute-start.4 = (bf16[512,3968]{1,0:T(8,128)(2,1)}, bf16[512,3968]{1,0:T(8,128)(2,1)}, u32[]{:S(2)}, u32[]{:S(2)}) collective-permute-start(bf16[512,3968]{1,0:T(8,128)(2,1)} %get-tuple-element.305), channel_id=1, source_target_pairs={{0,1},{1,0},{2,3},{3,2},{4,5},{5,4},{6,7},{7,6},{8,9},{9,8},{10,11... | collective-permute-start | bytes 12189704 | tf_op jit(solution)/shard_map/ppermute | solution.py:140
  972.8 65.8 %collective-permute-start.8 = (bf16[256,768]{1,0:T(8,128)(2,1)S(1)}, bf16[256,768]{1,0:T(8,128)(2,1)S(1)}, u32[]{:S(2)}, u32[]{:S(2)}) collective-permute-start(bf16[256,768]{1,0:T(8,128)(2,1)S(1)} %pad_maximum_fusion.10), channel_id=1, source_target_pairs={{0,2},{2,0},{4,6},{6,4},{8,10},{10,8},{12,14},{14,12},{16,18},{18,... | collective-permute-start | bytes 1179656 | tf_op jit(solution)/shard_map/ppermute | solution.py:140
  1125.2 59.5 %collective-permute-start.10 = (bf16[768,1152]{1,0:T(8,128)(2,1)}, bf16[768,1152]{1,0:T(8,128)(2,1)}, u32[]{:S(2)}, u32[]{:S(2)}) collective-permute-start(bf16[768,1152]{1,0:T(8,128)(2,1)} %convolution_convert_fusion.2), channel_id=1, source_target_pairs={{0,1},{1,0},{2,3},{3,2},{4,5},{5,4},{6,7},{7,6},{8,9},{9,8},{10,11... | collective-permute-start | bytes 5308424 | tf_op jit(solution)/shard_map/ppermute | solution.py:140
  1127.1 17.4 %collective-permute-start.19 = (bf16[768,384]{1,0:T(8,128)(2,1)}, bf16[768,384]{1,0:T(8,128)(2,1)}, u32[]{:S(2)}, u32[]{:S(2)}) collective-permute-start(bf16[768,384]{1,0:T(8,128)(2,1)} %convolution_convert_fusion.6), channel_id=1, source_target_pairs={{0,1},{1,0},{2,3},{3,2},{4,5},{5,4},{6,7},{7,6},{8,9},{9,8},{10,11... | collective-permute-start | bytes 1769480 | tf_op jit(solution)/shard_map/ppermute | solution.py:140
  1130.2 135.6 %collective-permute-start.28 = (bf16[768,1536]{1,0:T(8,128)(2,1)}, bf16[768,1536]{1,0:T(8,128)(2,1)}, u32[]{:S(2)}, u32[]{:S(2)}) collective-permute-start(bf16[768,1536]{1,0:T(8,128)(2,1)} %convolution_convert_fusion.1), channel_id=1, source_target_pairs={{0,1},{1,0},{2,3},{3,2},{4,5},{5,4},{6,7},{7,6},{8,9},{9,8},{10,11... | collective-permute-start | bytes 7077896 | tf_op jit(solution)/shard_map/ppermute | solution.py:140
  1151.9 16.6 %collective-permute-start.20 = (bf16[8,48,384]{2,1,0:T(8,128)(2,1)S(1)}, bf16[8,48,384]{2,1,0:T(8,128)(2,1)S(1)}, u32[]{:S(2)}, u32[]{:S(2)}) collective-permute-start(bf16[8,48,384]{2,1,0:T(8,128)(2,1)S(1)} %slice.380), channel_id=1, source_target_pairs={{0,2},{2,0},{4,6},{6,4},{8,10},{10,8},{12,14},{14,12},{16,18},{18,... | collective-permute-start | bytes 884744 | tf_op jit(solution)/shard_map/ppermute | solution.py:140
  1181.1 15.9 %collective-permute-start.23 = (bf16[1,48,384]{2,1,0:T(8,128)(2,1)}, bf16[1,48,384]{2,1,0:T(8,128)(2,1)}, u32[]{:S(2)}, u32[]{:S(2)}) collective-permute-start(bf16[1,48,384]{2,1,0:T(8,128)(2,1)} %slice.386), channel_id=1, source_target_pairs={{0,16},{2,18},{4,20},{6,22},{8,24},{10,26},{12,28},{14,30},{16,0},... | collective-permute-start | bytes 110600 | tf_op jit(solution)/shard_map/ppermute | solution.py:140
  1196.4 65.4 %collective-permute-start.11 = (bf16[8,48,1152]{2,1,0:T(8,128)(2,1)}, bf16[8,48,1152]{2,1,0:T(8,128)(2,1)}, u32[]{:S(2)}, u32[]{:S(2)}) collective-permute-start(bf16[8,48,1152]{2,1,0:T(8,128)(2,1)} %slice.376), channel_id=1, source_target_pairs={{0,2},{2,0},{4,6},{6,4},{8,10},{10,8},{12,14},{14,12},{16,18},{18,... | collective-permute-start | bytes 2654216 | tf_op jit(solution)/shard_map/ppermute | solution.py:140
  1198.5 53.4 %collective-permute-start.24 = (bf16[1,48,384]{2,1,0:T(8,128)(2,1)}, bf16[1,48,384]{2,1,0:T(8,128)(2,1)}, u32[]{:S(2)}, u32[]{:S(2)}) collective-permute-start(bf16[1,48,384]{2,1,0:T(8,128)(2,1)} %get-tuple-element.273), channel_id=1, source_target_pairs={{0,16},{2,18},{4,20},{6,22},{8,24},{10,26},{12,28},{14,30},{16,0},... | collective-permute-start | bytes 110600 | tf_op jit(solution)/shard_map/ppermute | solution.py:140
  1258.6 23.8 %collective-permute-start.26 = (bf16[4,48,384]{2,1,0:T(8,128)(2,1)}, bf16[4,48,384]{2,1,0:T(8,128)(2,1)}, u32[]{:S(2)}, u32[]{:S(2)}) collective-permute-start(bf16[4,48,384]{2,1,0:T(8,128)(2,1)} %pad_maximum_fusion.16), channel_id=1, source_target_pairs={{0,4},{2,6},{4,0},{6,2},{8,12},{10,14},{12,8},{14,10},{16,20},{18,... | collective-permute-start | bytes 442376 | tf_op jit(solution)/shard_map/ppermute | solution.py:140
  1265.8 14.7 %collective-permute-start.12 = (bf16[4,48,1152]{2,1,0:T(8,128)(2,1)}, bf16[4,48,1152]{2,1,0:T(8,128)(2,1)}, u32[]{:S(2)}, u32[]{:S(2)}) collective-permute-start(bf16[4,48,1152]{2,1,0:T(8,128)(2,1)} %slice.378), channel_id=1, source_target_pairs={{0,4},{2,6},{4,0},{6,2},{8,12},{10,14},{12,8},{14,10},{16,20},{18,... | collective-permute-start | bytes 1327112 | tf_op jit(solution)/shard_map/ppermute | solution.py:140
  1278.7 28.2 %collective-permute-start.29 = (bf16[8,48,1536]{2,1,0:T(8,128)(2,1)S(1)}, bf16[8,48,1536]{2,1,0:T(8,128)(2,1)S(1)}, u32[]{:S(2)}, u32[]{:S(2)}) collective-permute-start(bf16[8,48,1536]{2,1,0:T(8,128)(2,1)S(1)} %slice.375), channel_id=1, source_target_pairs={{0,2},{2,0},{4,6},{6,4},{8,10},{10,8},{12,14},{14,12},{16,18},{18,... | collective-permute-start | bytes 3538952 | tf_op jit(solution)/shard_map/ppermute | solution.py:140
  1283.4 27.8 %collective-permute-start.27 = (bf16[8,48,384]{2,1,0:T(8,128)(2,1)S(1)}, bf16[8,48,384]{2,1,0:T(8,128)(2,1)S(1)}, u32[]{:S(2)}, u32[]{:S(2)}) collective-permute-start(bf16[8,48,384]{2,1,0:T(8,128)(2,1)S(1)} %pad_maximum_fusion.11), channel_id=1, source_target_pairs={{0,2},{2,0},{4,6},{6,4},{8,10},{10,8},{12,14},{14,12},{16,18},{18,... | collective-permute-start | bytes 884744 | tf_op jit(solution)/shard_map/ppermute | solution.py:140
  1288.4 26.1 %collective-permute-start.14 = (bf16[1,48,1152]{2,1,0:T(8,128)(2,1)}, bf16[1,48,1152]{2,1,0:T(8,128)(2,1)}, u32[]{:S(2)}, u32[]{:S(2)}) collective-permute-start(bf16[1,48,1152]{2,1,0:T(8,128)(2,1)} %slice.384), channel_id=1, source_target_pairs={{0,16},{2,18},{4,20},{6,22},{8,24},{10,26},{12,28},{14,30},{16,0},... | collective-permute-start | bytes 331784 | tf_op jit(solution)/shard_map/ppermute | solution.py:140
  1323.3 15.9 %collective-permute-start.16 = (bf16[2,48,1152]{2,1,0:T(8,128)(2,1)S(1)}, bf16[2,48,1152]{2,1,0:T(8,128)(2,1)S(1)}, u32[]{:S(2)}, u32[]{:S(2)}) collective-permute-start(bf16[2,48,1152]{2,1,0:T(8,128)(2,1)S(1)} %pad_maximum_fusion.14), channel_id=1, source_target_pairs={{0,8},{2,10},{4,12},{6,14},{8,0},{10,2},{12,4},{14,6},{16,24},{18,... | collective-permute-start | bytes 663560 | tf_op jit(solution)/shard_map/ppermute | solution.py:140
  1350.3 18.4 %collective-permute-start.18 = (bf16[8,48,1152]{2,1,0:T(8,128)(2,1)S(1)}, bf16[8,48,1152]{2,1,0:T(8,128)(2,1)S(1)}, u32[]{:S(2)}, u32[]{:S(2)}) collective-permute-start(bf16[8,48,1152]{2,1,0:T(8,128)(2,1)S(1)} %pad_maximum_fusion.6), channel_id=1, source_target_pairs={{0,2},{2,0},{4,6},{6,4},{8,10},{10,8},{12,14},{14,12},{16,18},{18,... | collective-permute-start | bytes 2654216 | tf_op jit(solution)/shard_map/ppermute | solution.py:140
  1362.4 26.5 %collective-permute-start.36 = (bf16[8,48,1536]{2,1,0:T(8,128)(2,1)}, bf16[8,48,1536]{2,1,0:T(8,128)(2,1)}, u32[]{:S(2)}, u32[]{:S(2)}) collective-permute-start(bf16[8,48,1536]{2,1,0:T(8,128)(2,1)} %pad_maximum_fusion.4), channel_id=1, source_target_pairs={{0,2},{2,0},{4,6},{6,4},{8,10},{10,8},{12,14},{14,12},{16,18},{18,... | collective-permute-start | bytes 3538952 | tf_op jit(solution)/shard_map/ppermute | solution.py:140
  (147 other events, 1062.1 us)
Sparse Core Ops, SparseCore 0:
  9.6 10.6 all-gather.10
  21.8 13.8 all-gather.8
  37.2 15.7 all-gather.12
  98.7 15.8 all-gather.14

commit v2 on v0

v2 whole, which is shorter than its diff:
```python
import functools
import math

import jax
import jax.numpy as jnp
from jax import lax
from jax.experimental import pallas as pl
from jax.experimental.pallas import tpu as pltpu
from jax.sharding import PartitionSpec as P

D = 768
HEADS = 12
FF = 3072
ILEN = 145
LOWLEN = 50
CAP = 16

SCALE = 100.0
EPS = 1e-06
NEGATIVE = -1e30
LOG2E = math.log2(math.e)
MOST_PAIRS = 2048
VMEM_BYTES = 58 * 1024 * 1024

UNIT = 160
UNITS = 2
PART = 48
SPAN = 29
QB = 128
BW = 3 * D // 2 + D // 2 + 128
EARLY = D + 128
CHUNKS = 16

f32 = jnp.float32
bf16 = jnp.bfloat16


def dot(left_side, right_side):
    return jnp.dot(left_side, right_side, preferred_element_type=f32)


def dot_nt(left_side, right_side):
    return lax.dot_general(
        left_side, right_side, (((1,), (1,)), ((), ())), preferred_element_type=f32
    )


def dot_tn(left_side, right_side):
    return lax.dot_general(
        left_side, right_side, (((0,), (0,)), ((), ())), preferred_element_type=f32
    )


def normalize(values):
    center = values - jnp.mean(values, -1, keepdims=True)
    inverse = lax.rsqrt(jnp.mean(center * center, -1, keepdims=True) + EPS)
    return center * inverse, inverse


def norm_back(grad, normed, inverse):
    return inverse * (
        grad
        - jnp.mean(grad, -1, keepdims=True)
        - normed * jnp.mean(grad * normed, -1, keepdims=True)
    )


def normal_cdf(values):
    return 0.5 + 0.5 * lax.erf(values * (1.0 / math.sqrt(2.0)))


def split_low(values):
    big = values.astype(bf16)
    return big, (values - big.astype(f32)).astype(bf16)


def tower_kernel(
    groups_ref,
    mine_ref,
    x_hbm,
    vec_own_ref,
    vec_other_ref,
    qkv_own,
    qkv_other,
    out_own,
    out_other,
    up_own,
    up_other,
    down_own,
    down_other,
    emb_ref,
    order,
    x_ref,
    x_wide,
    wqkv,
    wout,
    wup,
    wdown,
    gain_a,
    bqkv,
    gain_m,
    bup,
    xs,
    qkv,
    mixed,
    asum,
    hsum,
    aparts,
    hparts,
    sems,
):
    total = x_ref.shape[1]
    pitch = total + 8
    mine = mine_ref[0]
    copies = []
    for k in range(ILEN // SPAN):
        span = pl.ds(k * SPAN, SPAN)
        copies.append(pltpu.make_async_copy(x_hbm.at[span], x_ref.at[span], sems.at[8 + k]))
    for k, (own, other, whole) in enumerate(
        (
            (qkv_own, qkv_other, wqkv),
            (out_own, out_other, wout),
            (up_own, up_other, wup),
            (down_own, down_other, wdown),
        )
    ):
        half = own.shape[0]
        copies.append(
            pltpu.make_async_copy(own, whole.at[pl.ds(mine * half, half)], sems.at[2 * k])
        )
        copies.append(
            pltpu.make_async_copy(
                other, whole.at[pl.ds((1 - mine) * half, half)], sems.at[2 * k + 1]
            )
        )
    for copy in copies:
        copy.start()

    vec_own = vec_own_ref[...].astype(f32)
    vec_other = vec_other_ref[...].astype(f32)
    low = jnp.where(mine == 0, vec_own, vec_other)
    high = jnp.where(mine == 0, vec_other, vec_own)
    start = 0
    for dest, size, at in (
        (gain_a, D // 2, (0, D // 2)),
        (bqkv, D, (0, 2 * D)),
        (gain_m, D // 2, (0, D // 2)),
        (bup, FF // 2, (0, FF // 2)),
    ):
        dest[:, at[0] : at[0] + size] = low[:, start : start + size]
        dest[:, at[1] : at[1] + size] = high[:, start : start + size]
        start += size
    bqkv[:, D : 2 * D] = jnp.zeros((1, D), f32)

    def count(i, found):
        return found + groups_ref[i]

    n_hi = lax.fori_loop(0, total, count, 0)

    def place_one(i, state):
        hi, lo = state
        group = groups_ref[i]
        order[jnp.where(group == 1, hi, lo)] = i
        return hi + group, lo + 1 - group

    lax.fori_loop(0, total, place_one, (0, n_hi))
    n_units = n_hi + (total - n_hi + 2) // 3

    xs[...] = jnp.zeros_like(xs)
    first = lax.broadcasted_iota(jnp.int32, (1, 128), 1) < 64
    key_at = lax.broadcasted_iota(jnp.int32, (UNIT, UNIT), 1)
    row_at = lax.broadcasted_iota(jnp.int32, (UNIT, UNIT), 0)
    sub = lax.broadcasted_iota(jnp.int32, (8, 1), 0)

    def place(unit, k):
        last = jnp.minimum(unit, n_units - 1)
        is_hi = last < n_hi
        where = jnp.where(is_hi, last, n_hi + 3 * (last - n_hi) + k)
        return order[jnp.minimum(where, total - 1)], is_hi

    def keep_parts(values, j, dest, col, width):
        rows = values.reshape(UNIT // 8, 8, width)
        parts = [
            jnp.sum(rows[0:6], 0),
            rows[6],
            jnp.sum(rows[7:12], 0),
            rows[12],
            jnp.sum(rows[13:18], 0),
            rows[18],
        ]
        for k, part in enumerate(parts):
            dest[j * PART + k * 8 : j * PART + k * 8 + 8, col : col + width] = part

    loads = copies[: ILEN // SPAN]
    copies = copies[ILEN // SPAN :]

    def widen(t, carry):
        for panel in range(D // 128):
            x_wide[panel, pl.ds(pl.multiple_of(t * pitch, 8), total), :] = x_ref[
                t, :, panel * 128 : (panel + 1) * 128
            ].astype(f32)
        return carry

    for k, load in enumerate(loads):
        load.wait()
        lax.fori_loop(k * SPAN, (k + 1) * SPAN, widen, 0)
    for copy in copies[:2]:
        copy.wait()

    def body(step, carry):
        for j in range(UNITS):
            unit = step * UNITS + j
            one, is_hi = place(unit, 0)
            two, three = place(unit, 1)[0], place(unit, 2)[0]
            base = j * UNIT

            @pl.when(is_hi)
            def _():
                for panel in range(D // 128):
                    xs[base : base + ILEN, panel * 128 : (panel + 1) * 128] = x_wide[
                        panel, pl.ds(one, ILEN, stride=pitch), :
                    ]

            @pl.when(jnp.logical_not(is_hi))
            def _():
                for k, index in enumerate((one, two, three)):
                    for panel in range(D // 128):
                        xs[
                            base + LOWLEN * k : base + LOWLEN * (k + 1),
                            panel * 128 : (panel + 1) * 128,
                        ] = x_wide[panel, pl.ds(index, LOWLEN, stride=pitch), :]

        low_rows = (normalize(xs[...])[0] * gain_a[...]).astype(bf16)
        for col in range(0, 3 * D, 256):
            values = dot(low_rows, wqkv[:, col : col + 256]) + bqkv[:, col : col + 256]
            if col < D:
                values = values * (LOG2E / 8.0)
            qkv[:, col : col + 256] = values.astype(bf16)

        @pl.when(step == 0)
        def _():
            for copy in copies[2:6]:
                copy.wait()

        for j in range(UNITS):
            is_hi = place(step * UNITS + j, 0)[1]
            base = j * UNIT
            key_seg = jnp.where(key_at < LOWLEN, 0, jnp.where(key_at < 2 * LOWLEN, 1, 2))
            row_seg = jnp.where(row_at < LOWLEN, 0, jnp.where(row_at < 2 * LOWLEN, 1, 2))
            short_ok = jnp.logical_and(key_seg == row_seg, key_at < 3 * LOWLEN)
            allowed = jnp.where(
                is_hi, (key_at < ILEN).astype(jnp.int32), short_ok.astype(jnp.int32)
            )
            bias = jnp.where(allowed > 0, 0.0, NEGATIVE)
            for p in range(HEADS // 2):
                lanes = slice(p * 128, (p + 1) * 128)
                query = qkv[base : base + UNIT, lanes]
                key = qkv[base : base + UNIT, D + p * 128 : D + (p + 1) * 128]
                value = qkv[base : base + UNIT, 2 * D + p * 128 : 2 * D + (p + 1) * 128]
                value_one = jnp.concatenate([value, jnp.ones_like(value)], 1)
                outs = []
                for h in range(2):
                    head = first if h == 0 else jnp.logical_not(first)
                    scores = dot_nt(jnp.where(head, query, jnp.zeros_like(query)), key) + bias
                    powers = jnp.exp2(scores - jnp.max(scores, 1, keepdims=True)).astype(bf16)
                    summed = dot(powers, value_one)
                    outs.append(summed[:, :128] / summed[:, 128:])
                mixed[base : base + UNIT, lanes] = jnp.where(first, outs[0], outs[1]).astype(bf16)
        for col in range(0, D, 256):
            xs[:, col : col + 256] += dot(mixed[...], wout[:, col : col + 256])
        for j in range(UNITS):
            keep_parts(xs[j * UNIT : (j + 1) * UNIT, :], j, aparts, 0, D)
        low_two = (normalize(xs[...])[0] * gain_m[...]).astype(bf16)
        width = 1024
        for col in range(0, FF, width):
            pre_act = dot(low_two, wup[:, col : col + width]) + bup[:, col : col + width]
            hidden = pre_act * normal_cdf(pre_act)
            for j in range(UNITS):
                keep_parts(hidden[j * UNIT : (j + 1) * UNIT], j, hparts, col, width)
        for j in range(UNITS):
            unit = step * UNITS + j
            one, is_hi = place(unit, 0)
            two, three = place(unit, 1)[0], place(unit, 2)[0]

            def rows_of(index):
                return pl.ds(pl.multiple_of(index * 8, 8), 8)

            @pl.when(is_hi)
            def _():
                for src, dest in ((aparts, asum), (hparts, hsum)):
                    part = [src[j * PART + k * 8 : j * PART + k * 8 + 8, :] for k in range(6)]
                    dest[rows_of(one), :] = (
                        (part[0] + part[1])
                        + (part[2] + part[3])
                        + (part[4] + jnp.where(sub < 1, part[5], 0.0))
                    )

            @pl.when(jnp.logical_not(is_hi))
            def _():
                for src, dest in ((aparts, asum), (hparts, hsum)):
                    part = [src[j * PART + k * 8 : j * PART + k * 8 + 8, :] for k in range(6)]
                    dest[rows_of(three), :] = (
                        jnp.where(sub < 4, 0.0, part[3])
                        + part[4]
                        + jnp.where(sub < 6, part[5], 0.0)
                    )
                    dest[rows_of(two), :] = (
                        jnp.where(sub < 2, 0.0, part[1])
                        + part[2]
                        + jnp.where(sub < 4, part[3], 0.0)
                    )
                    dest[rows_of(one), :] = part[0] + jnp.where(sub < 2, part[1], 0.0)

        return carry

    lax.fori_loop(0, (n_units + UNITS - 1) // UNITS, body, 0)
    for copy in copies[6:]:
        copy.wait()
    which = lax.broadcasted_iota(jnp.int32, (total, 128), 0)
    scale = jnp.zeros((total, 128), f32)
    for i in range(total):
        scale = jnp.where(
            which == i, jnp.where(groups_ref[i] == 1, 1.0 / ILEN, 1.0 / LOWLEN), scale
        )
    scale = scale[:, 0:1]
    big, rest = split_low(jnp.sum(hsum[...].reshape(total, 8, FF), 1) * scale)
    product = dot(jnp.concatenate([big, rest], 0), wdown[...])
    pooled = jnp.sum(asum[...].reshape(total, 8, D), 1) * scale + product[:total] + product[total:]
    emb_ref[...] = (
        pooled * lax.rsqrt(jnp.sum(pooled * pooled, -1, keepdims=True) + EPS)
    ).astype(bf16)


VM = pl.BlockSpec(memory_space=pltpu.VMEM)
SM = pl.BlockSpec(memory_space=pltpu.SMEM)
ANY = pl.BlockSpec(memory_space=pl.ANY)
PARAMS = pltpu.CompilerParams(vmem_limit_bytes=VMEM_BYTES)


def image_tower(images, groups, mine, vec_own, vec_other, weights):
    number = images.shape[1]
    rows = UNITS * UNIT
    flops = number * 100 * 2 * (4 * D * D + D * FF)
    return pl.pallas_call(
        tower_kernel,
        out_shape=jax.ShapeDtypeStruct((number, D), bf16),
        in_specs=[SM, SM, ANY, VM, VM] + [ANY] * 8,
        out_specs=VM,
        scratch_shapes=[
            pltpu.SMEM((number,), jnp.int32),
            pltpu.VMEM(images.shape, bf16),
            pltpu.VMEM((D // 128, ILEN * (number + 8), 128), f32),
            pltpu.VMEM((D, 3 * D), bf16),
            pltpu.VMEM((D, D), bf16),
            pltpu.VMEM((D, FF), bf16),
            pltpu.VMEM((FF, D), bf16),
            pltpu.VMEM((1, D), f32),
            pltpu.VMEM((1, 3 * D), f32),
            pltpu.VMEM((1, D), f32),
            pltpu.VMEM((1, FF), f32),
            pltpu.VMEM((rows, D), f32),
            pltpu.VMEM((rows, 3 * D), bf16),
            pltpu.VMEM((rows, D), bf16),
            pltpu.VMEM((number * 8, D), f32),
            pltpu.VMEM((number * 8, FF), f32),
            pltpu.VMEM((UNITS * PART, D), f32),
            pltpu.VMEM((UNITS * PART, FF), f32),
            pltpu.SemaphoreType.DMA((8 + ILEN // SPAN,)),
        ],
        compiler_params=PARAMS,
        cost_estimate=pl.CostEstimate(
            flops=flops, bytes_accessed=24 * 1024 * 1024, transcendentals=0
        ),
        name="image_tower",
    )(groups, mine, images, vec_own, vec_other, *weights)


def lens_along(lens_ref, start, number):
    owner = lax.broadcasted_iota(jnp.int32, (1, number * CAP), 1) // CAP
    lens = jnp.zeros((1, number * CAP), jnp.int32)
    for c in range(number):
        lens = jnp.where(owner == c, lens_ref[start + c], lens)
    return lens


def score_bias(lens_ref, block):
    per = QB // CAP
    position = lax.broadcasted_iota(jnp.int32, (1, QB), 1) % CAP
    valid = position < lens_along(lens_ref, block * per, per)
    rows = lax.broadcasted_iota(jnp.int32, (QB, QB), 0) // CAP
    columns = lax.broadcasted_iota(jnp.int32, (QB, QB), 1) // CAP
    return jnp.where(jnp.logical_and(rows == columns, valid), 0.0, NEGATIVE)


def forward_kernel(
    lens_ref,
    x_ref,
    vec_ref,
    wqkv_ref,
    wout_ref,
    wup_ref,
    wdown_ref,
    qkv,
    mixed,
    after,
    mlp,
    slope,
    early,
    hidden_low,
    hidden,
):
    rows = x_ref.shape[0]
    number = rows // CAP
    first = lax.broadcasted_iota(jnp.int32, (1, 128), 1) < 64
    normed, _ = normalize(x_ref[...].astype(f32))
    low = (normed * vec_ref[:, 0:D]).astype(bf16)
    for col in range(0, 3 * D, 256):
        values = dot(low, wqkv_ref[:, col : col + 256])
        if col < D:
            values = values + vec_ref[:, D + col : D + col + 256]
        if col >= 2 * D:
            values = values + vec_ref[:, col : col + 256]
        values = values.astype(bf16)
        if col < D:
            values = values * jnp.asarray(0.125, bf16)
        qkv[:, col : col + 256] = values
    def one_block(block, carry):
        bias = score_bias(lens_ref, block)
        span = pl.ds(pl.multiple_of(block * QB, QB), QB)
        for p in range(HEADS // 2):
            query = qkv[span, p * 128 : (p + 1) * 128]
            key = qkv[span, D + p * 128 : D + (p + 1) * 128]
            value = qkv[span, 2 * D + p * 128 : 2 * D + (p + 1) * 128]
            value_one = jnp.concatenate([value, jnp.ones_like(value)], 1)
            outs = []
            for h in range(2):
                head = first if h == 0 else jnp.logical_not(first)
                scores = dot_nt(jnp.where(head, query, jnp.zeros_like(query)), key) * LOG2E + bias
                powers = jnp.exp2(scores - jnp.max(scores, 1, keepdims=True)).astype(bf16)
                summed = dot(powers, value_one)
                outs.append(summed[:, :128] / summed[:, 128:])
            mixed[span, p * 128 : (p + 1) * 128] = jnp.where(first, outs[0], outs[1]).astype(bf16)
        return carry

    lax.fori_loop(0, rows // QB, one_block, 0)
    for col in range(0, D, 256):
        after[:, col : col + 256] = x_ref[:, col : col + 256].astype(f32) + dot(
            mixed[...], wout_ref[:, col : col + 256]
        )
    mlp[...] = (normalize(after[...])[0] * vec_ref[:, 3 * D : 4 * D]).astype(bf16)
    lens = lens_along(lens_ref, 0, number)
    position = lax.broadcasted_iota(jnp.int32, (1, rows), 1)
    owner = (
        lax.broadcasted_iota(jnp.int32, (number, rows), 0)
        == lax.broadcasted_iota(jnp.int32, (number, rows), 1) // CAP
    )
    members = jnp.where(jnp.logical_and(owner, position % CAP < lens), 1.0, 0.0)
    pool = members.astype(bf16)
    count = jnp.sum(members, 1, keepdims=True)
    width = 512
    for col in range(0, FF, width):
        span = slice(col, col + width)
        pre_act = dot(mlp[...], wup_ref[:, span]) + vec_ref[:, 4 * D + col : 4 * D + col + width]
        phi = normal_cdf(pre_act)
        hidden[:, span] = (pre_act * phi).astype(bf16)
        density = jnp.exp2(pre_act * pre_act * (-0.5 * LOG2E)) * (1.0 / math.sqrt(2.0 * math.pi))
        slope[:, span] = (phi + pre_act * density).astype(bf16)
    big, rest = split_low(dot(pool, hidden[...]))
    after_big, after_rest = split_low(after[...])
    pooled = (
        dot(pool, after_big)
        + dot(pool, after_rest)
        + dot(big, wdown_ref[...])
        + dot(rest, wdown_ref[...])
    )
    early[:, 0:D] = (pooled / count).astype(bf16)
    early[:, D:EARLY] = jnp.broadcast_to(count, (number, EARLY - D)).astype(bf16)
    hidden_low[...] = big


def text_forward(captions, lens, vec, w_qkv, w_out, w_up, w_down):
    rows = captions.shape[0]
    shape = jax.ShapeDtypeStruct
    return pl.pallas_call(
        forward_kernel,
        out_shape=[
            shape((rows, 3 * D), bf16),
            shape((rows, D), bf16),
            shape((rows, D), f32),
            shape((rows, D), bf16),
            shape((rows, FF), bf16),
            shape((rows // CAP, EARLY), bf16),
            shape((rows // CAP, FF), bf16),
        ],
        in_specs=[SM] + [VM] * 6,
        out_specs=[VM] * 7,
        scratch_shapes=[pltpu.VMEM((rows, FF), bf16)],
        compiler_params=PARAMS,
        cost_estimate=pl.CostEstimate(
            flops=2 * rows * (4 * D * D + 2 * D * FF),
            bytes_accessed=24 * 1024 * 1024,
            transcendentals=0,
        ),
        name="text_forward",
    )(lens, captions, vec, w_qkv, w_out, w_up, w_down)


def put_chunks(dest, values, place_ref, stream, col):
    rows = values.shape[0] // CHUNKS
    for chunk in range(CHUNKS):
        at = pl.multiple_of(place_ref[stream, chunk] * rows, 16)
        dest[pl.ds(at, rows), col : col + values.shape[1]] = values[
            chunk * rows : (chunk + 1) * rows
        ].astype(dest.dtype)


def up_kernel(
    place_ref, mine_ref, lens_ref, branch_ref, slope_ref, mlp_ref, wdown_ref,
    grad_pre, own, other, grad_bup, grad_hidden, mlp_t,
):
    number = slope_ref.shape[0] // CAP
    half = FF // 2
    mine = mine_ref[0]
    for col in range(0, FF, 512):
        grad_hidden[:, col : col + 512] = dot_nt(branch_ref[...], wdown_ref[col : col + 512, :])
    position = lax.broadcasted_iota(jnp.int32, (CAP, 1), 0)
    for c in range(number):
        span = slice(c * CAP, (c + 1) * CAP)
        keep = jnp.where(position < lens_ref[c], 1.0, 0.0)
        grad_pre[span, :] = (
            grad_hidden[c : c + 1, :] * slope_ref[span, :].astype(f32) * keep
        ).astype(bf16)
    mlp_t[...] = mlp_ref[...].T
    for which, dest in ((1 - mine, other), (mine, own)):
        for col in range(0, half, 384):
            lanes = pl.ds(pl.multiple_of(which * half + col, 128), 384)
            put_chunks(dest, dot(mlp_t[...], grad_pre[:, lanes]), place_ref, 2 * col // half, col)
    for col in range(0, FF, 512):
        grad_bup[:, col : col + 512] = jnp.sum(
            grad_pre[:, col : col + 512].astype(f32), 0, keepdims=True
        )


def up_backward(place, mine, lens, branch, slope, mlp, w_down):
    rows = slope.shape[0]
    shape = jax.ShapeDtypeStruct
    return pl.pallas_call(
        up_kernel,
        out_shape=[
            shape((rows, FF), bf16),
            shape((D, FF // 2), f32),
            shape((D, FF // 2), bf16),
            shape((1, FF), f32),
        ],
        in_specs=[SM, SM, SM] + [VM] * 4,
        out_specs=[VM] * 4,
        scratch_shapes=[pltpu.VMEM((rows // CAP, FF), f32), pltpu.VMEM((D, rows), bf16)],
        compiler_params=PARAMS,
        cost_estimate=pl.CostEstimate(
            flops=2 * rows * D * FF, bytes_accessed=20 * 1024 * 1024, transcendentals=0
        ),
        name="up_backward",
    )(place, mine, lens, branch, slope, mlp, w_down)


def mlp_kernel(
    lens_ref, pre_ref, grad_ref, after_ref, vec_ref, wup_ref, wout_ref,
    grad_after, grad_mixed, grad_gain, grad_out,
):
    number = after_ref.shape[0] // CAP
    grad_mlp = dot_nt(pre_ref[...], wup_ref[...])
    normed_two, inverse_two = normalize(after_ref[...])
    grad_gain[...] = jnp.sum(grad_mlp * normed_two, 0, keepdims=True)
    grad_after[...] = norm_back(grad_mlp * vec_ref[:, 3 * D : 4 * D], normed_two, inverse_two)
    position = lax.broadcasted_iota(jnp.int32, (CAP, 1), 0)
    for c in range(number):
        keep = jnp.where(position < lens_ref[c], 1.0, 0.0)
        grad_after[c * CAP : (c + 1) * CAP, :] += grad_ref[c : c + 1, :] * keep
    grad_out[...] = grad_after[...].astype(bf16)
    for col in range(0, D, 256):
        grad_mixed[:, col : col + 256] = dot_nt(
            grad_out[...], wout_ref[col : col + 256, :]
        ).astype(bf16)


def mlp_backward(lens, grad_pre, grads, after, vec, w_up, w_out):
    rows = after.shape[0]
    shape = jax.ShapeDtypeStruct
    return pl.pallas_call(
        mlp_kernel,
        out_shape=[shape((rows, D), f32), shape((rows, D), bf16), shape((1, D), f32)],
        in_specs=[SM] + [VM] * 6,
        out_specs=[VM] * 3,
        scratch_shapes=[pltpu.VMEM((rows, D), bf16)],
        compiler_params=PARAMS,
        cost_estimate=pl.CostEstimate(
            flops=2 * rows * (D * D + D * FF), bytes_accessed=20 * 1024 * 1024, transcendentals=0
        ),
        name="mlp_backward",
    )(lens, grad_pre, grads, after, vec, w_up, w_out)


def attention_kernel(lens_ref, qkv_ref, mixed_ref, grad_proj, *, start):
    blocks = grad_proj.shape[0] // QB
    first = lax.broadcasted_iota(jnp.int32, (1, 128), 1) < 64

    def one_block(block, carry):
        bias = score_bias(lens_ref, start // QB + block)
        span = pl.ds(pl.multiple_of(start + block * QB, QB), QB)
        dest = pl.ds(pl.multiple_of(block * QB, QB), QB)
        for p in range(HEADS // 2):
            at = p * 128
            query = qkv_ref[span, at : at + 128]
            key = qkv_ref[span, D + at : D + at + 128]
            value = qkv_ref[span, 2 * D + at : 2 * D + at + 128]
            grad = mixed_ref[span, at : at + 128]
            grad_q, grad_k, grad_v = [], [], []
            for h in range(2):
                head = first if h == 0 else jnp.logical_not(first)
                scores = dot_nt(jnp.where(head, query, jnp.zeros_like(query)), key) * LOG2E + bias
                powers = jnp.exp2(scores - jnp.max(scores, 1, keepdims=True))
                attention = powers / jnp.sum(powers, 1, keepdims=True)
                grad_att = dot_nt(jnp.where(head, grad, jnp.zeros_like(grad)), value)
                grad_s = (
                    attention * (grad_att - jnp.sum(grad_att * attention, 1, keepdims=True))
                ).astype(bf16)
                grad_q.append(dot(grad_s, key))
                grad_k.append(dot_tn(grad_s, query))
                grad_v.append(dot_tn(attention.astype(bf16), grad))
            for k, (parts, scale) in enumerate(((grad_q, 0.125), (grad_k, 1.0), (grad_v, 1.0))):
                grad_proj[dest, k * D + at : k * D + at + 128] = (
                    jnp.where(first, parts[0], parts[1]) * scale
                ).astype(bf16)
        return carry

    lax.fori_loop(0, blocks, one_block, 0)


def attention_backward(lens, qkv, grad_mixed, start, rows):
    return pl.pallas_call(
        functools.partial(attention_kernel, start=start),
        out_shape=jax.ShapeDtypeStruct((rows, 3 * D), bf16),
        in_specs=[SM] + [VM] * 2,
        out_specs=VM,
        compiler_params=PARAMS,
        cost_estimate=pl.CostEstimate(
            flops=2 * rows * 3 * D * D, bytes_accessed=16 * 1024 * 1024, transcendentals=0
        ),
        name="attention_backward",
    )(lens, qkv, grad_mixed)


def proj_kernel(
    place_ref, mine_ref, proj_low, proj_high, after_ref, mixed_ref, x_ref, vec_ref,
    gain_ref, bup_ref, wqkv_ref,
    caption_grad, own, other, grad_proj, sums, lhs_t, grad_out,
):
    half_rows = proj_low.shape[0]
    chunk_rows = D // CHUNKS
    mine = mine_ref[0]
    gain_a = vec_ref[:, 0:D]
    grad_proj[0:half_rows, :] = proj_low[...]
    grad_proj[half_rows:, :] = proj_high[...]
    normed_one, inverse_one = normalize(x_ref[...].astype(f32))
    lhs_t[...] = (normed_one * gain_a).astype(bf16).T
    half_out, half_qkv = D // 2, 3 * D // 2
    for which, dest in ((1 - mine, other), (mine, own)):
        for col in range(0, half_qkv, 384):
            lanes = pl.ds(pl.multiple_of(which * half_qkv + col, 128), 384)
            put_chunks(dest, dot(lhs_t[...], grad_proj[:, lanes]), place_ref, col // 768, col)
    lhs_t[...] = mixed_ref[...].T
    grad_out[...] = after_ref[...].astype(bf16)
    for which, dest in ((1 - mine, other), (mine, own)):
        lanes = pl.ds(pl.multiple_of(which * half_out, 128), half_out)
        put_chunks(dest, dot(lhs_t[...], grad_out[:, lanes]), place_ref, 1, half_qkv)
    grad_in = dot_nt(grad_proj[...], wqkv_ref[...])
    sums[:, 0:D] = jnp.sum(grad_in * normed_one, 0, keepdims=True)
    sums[:, D : 2 * D] = jnp.sum(grad_proj[:, 0:D].astype(f32), 0, keepdims=True)
    sums[:, 2 * D : 3 * D] = jnp.sum(grad_proj[:, 2 * D :].astype(f32), 0, keepdims=True)
    sums[:, 3 * D : 4 * D] = gain_ref[...]
    sums[:, 4 * D :] = bup_ref[...]
    caption_grad[...] = after_ref[...] + norm_back(grad_in * gain_a, normed_one, inverse_one)
    for which, dest in ((1 - mine, other), (mine, own)):
        dest[:, BW - 128 :] = jnp.zeros((D, 128), dest.dtype)
        pieces = []
        for start, size in ((0, D), (D, 2 * D), (3 * D, D), (4 * D, FF)):
            for k in range(0, size // 2, 128):
                at = pl.multiple_of(start + which * (size // 2) + k, 128)
                pieces.append(sums[:, pl.ds(at, 128)])
        pieces += [jnp.zeros_like(pieces[0])] * (32 - len(pieces))
        at = pl.multiple_of(place_ref[1, 0] * chunk_rows, 16)
        dest[pl.ds(at, 32), BW - 128 :] = jnp.concatenate(pieces, 0).astype(dest.dtype)


def proj_backward(
    place, mine, proj_low, proj_high, grad_after, mixed, captions, vec, grad_gain, grad_bup, w_qkv
):
    rows = captions.shape[0]
    shape = jax.ShapeDtypeStruct
    return pl.pallas_call(
        proj_kernel,
        out_shape=[shape((rows, D), f32), shape((D, BW), f32), shape((D, BW), bf16)],
        in_specs=[SM, SM] + [VM] * 9,
        out_specs=[VM] * 3,
        scratch_shapes=[
            pltpu.VMEM((rows, 3 * D), bf16),
            pltpu.VMEM((1, 4 * D + FF), f32),
            pltpu.VMEM((D, rows), bf16),
            pltpu.VMEM((rows, D), bf16),
        ],
        compiler_params=PARAMS,
        cost_estimate=pl.CostEstimate(
            flops=2 * rows * 7 * D * D, bytes_accessed=20 * 1024 * 1024, transcendentals=0
        ),
        name="proj_backward",
    )(place, mine, proj_low, proj_high, grad_after, mixed, captions, vec, grad_gain, grad_bup, w_qkv)


def dp_bits():
    bits, bit = [], 1
    while bit < lax.axis_size("dp"):
        bits.append(bit)
        bit *= 2
    return bits


def swap(values, axis, bit):
    size = lax.axis_size(axis)
    return lax.ppermute(values, axis, [(place, place ^ bit) for place in range(size)])


def gather_relative(values):
    bits = dp_bits()
    while bits:
        pair = bits[-2:]
        bits = bits[:-2]
        offsets = [0]
        for bit in pair:
            offsets += [entry + bit for entry in offsets]
        values = jnp.concatenate([swap(values, "dp", k) if k else values for k in offsets], 0)
    return jnp.concatenate([values, swap(values, "rep", 1)], 0)


def relative_chips():
    bits, table = dp_bits(), [0]
    while bits:
        pair = bits[-2:]
        bits = bits[:-2]
        offsets = [0]
        for bit in pair:
            offsets += [entry + bit for entry in offsets]
        table = [entry ^ k for k in offsets for entry in table]
    return table


def chunk_places():
    away = jnp.arange(CHUNKS, dtype=jnp.int32) ^ (lax.axis_index("dp") % CHUNKS)
    one, two, rest = away % 2, away // 2 % 2, away // 4
    return jnp.stack([one * 8 + two * 4 + rest, two * 8 + one * 4 + rest]).astype(jnp.int32)


def reduce_chunks(own, arrived, first_width):
    half, quarter, last = (own.shape[0] // k for k in (2, 4, CHUNKS))
    streams = ((slice(0, first_width), 1, 2), (slice(first_width, None), 2, 1))

    def both(rows, lanes):
        return own[rows, lanes] + arrived[rows, lanes].astype(f32)

    came = [
        swap(both(slice(half, None), lanes).astype(bf16), "dp", bit) for lanes, bit, _ in streams
    ]
    kept = [
        both(slice(0, half), lanes) + got.astype(f32)
        for (lanes, _, _), got in zip(streams, came, strict=True)
    ]
    came = [
        swap(total[quarter:].astype(bf16), "dp", bit)
        for total, (_, _, bit) in zip(kept, streams, strict=True)
    ]
    total = jnp.concatenate(
        [kept[k][:quarter] + came[k].astype(f32) for k in range(2)], 1
    )
    parts = [
        swap(total[k * last : (k + 1) * last].astype(bf16), "dp", 4 * k) for k in (1, 2, 3)
    ]
    total = total[:last] + sum(part.astype(f32) for part in parts)
    for bit in dp_bits()[4:]:
        total = total + swap(total.astype(bf16), "dp", bit).astype(f32)
    return total.astype(bf16)


def spread_chunks(chunk, first_width):
    column = [swap(chunk, "dp", 4 * k) if k else chunk for k in range(4)]
    quarters = []
    for lanes, one, two in ((slice(0, first_width), 1, 2), (slice(first_width, None), 2, 1)):
        mine = jnp.concatenate([piece[:, lanes] for piece in column], 0)
        near = swap(mine, "dp", two)
        quarters += [mine, near, swap(mine, "dp", one), swap(near, "dp", one)]
    return quarters


def unpack_kernel(place_ref, *refs):
    parts = refs[:16]
    g_up, g_qkv, g_out = refs[16:19]
    vectors = refs[19:]
    rows = D // CHUNKS
    place = place_ref[0, 0]
    me = place // 8 + 2 * (place // 4 % 2) + 4 * (place % 4)
    for stream in range(2):
        for quarter in range(4):
            for k in range(4):
                high, low = quarter // 2, quarter % 2
                away = (high + 2 * low if stream == 0 else low + 2 * high) + 4 * k
                chunk = me ^ away
                at = pl.ds(pl.multiple_of(chunk * rows, 16), rows)
                span = slice(k * rows, (k + 1) * rows)
                lanes = slice(stream * FF // 4, (stream + 1) * FF // 4)
                g_up[at, lanes] = parts[stream * 4 + quarter][span, :].astype(f32)
                rest = parts[8 + stream * 4 + quarter][span, :].astype(f32)
                if stream == 0:
                    g_qkv[at, 0:D] = rest
                    continue
                g_qkv[at, D:] = rest[:, : D // 2]
                g_out[at, :] = rest[:, D // 2 : D]

                @pl.when(chunk == 0)
                def _():
                    row = 0
                    for dest in vectors:
                        for lane in range(0, dest.shape[0], 128):
                            dest[lane : lane + 128] = rest[row, D:]
                            row += 1


def unpack(place, ups, rests):
    shape = jax.ShapeDtypeStruct
    return pl.pallas_call(
        unpack_kernel,
        out_shape=[
            shape((D, FF // 2), f32),
            shape((D, 3 * D // 2), f32),
            shape((D, D // 2), f32),
            shape((D // 2,), f32),
            shape((D,), f32),
            shape((D // 2,), f32),
            shape((FF // 2,), f32),
        ],
        in_specs=[SM] + [VM] * 16,
        out_specs=[VM] * 7,
        compiler_params=PARAMS,
        name="unpack",
    )(place, *ups, *rests)


def softmax_parts(scores, axis):
    maxima = jnp.max(scores, axis, keepdims=True)
    powers = jnp.exp(scores - maxima)
    totals = jnp.sum(powers, axis, keepdims=True)
    return powers / totals, maxima + jnp.log(totals)


def text_unit(pooled_low, text_proj):
    proj_out = dot(pooled_low, text_proj)
    inverse_z = lax.rsqrt(jnp.sum(proj_out * proj_out, -1, keepdims=True) + EPS)
    return proj_out * inverse_z, inverse_z


def branch_grad(grad_unit, unit_text, inverse_z, text_proj, lengths):
    grad_projout = (
        inverse_z * (grad_unit - unit_text * jnp.sum(unit_text * grad_unit, -1, keepdims=True))
    ).astype(bf16)
    return dot_nt(grad_projout, text_proj) / lengths


def loss_whole(pooled_all, image_all, text_proj, lengths_all, same, first_row, local_pairs):
    unit_text, inverse_z = text_unit(pooled_all, text_proj)
    scores = dot_nt(unit_text.astype(bf16), image_all) * SCALE
    by_text, text_total = softmax_parts(scores, 1)
    by_image, image_total = softmax_parts(scores, 0)

    def own_rows(values):
        return lax.dynamic_slice_in_dim(values, first_row, local_pairs, 0)

    own = jnp.sum(own_rows(scores * same), -1)
    pair_loss = 0.5 * (own_rows(text_total)[:, 0] - own) + 0.5 * (
        image_total[0, :local_pairs] - own
    )
    sgrad = (0.5 * (by_text - same) + 0.5 * (by_image - same)).astype(bf16)
    grad_unit = dot(sgrad, image_all) * SCALE
    grads = branch_grad(grad_unit, unit_text, inverse_z, text_proj, lengths_all)
    return pair_loss, own_rows(grads), grads.astype(bf16)


def loss_rows(pooled_all, image_all, text_proj, lengths_all, same, first_row, local_pairs):
    unit_all, inverse_all = text_unit(pooled_all, text_proj)

    def own_rows(values):
        return lax.dynamic_slice_in_dim(values, first_row, local_pairs, 0)

    unit_text, inverse_z = own_rows(unit_all), own_rows(inverse_all)
    text_scores = dot_nt(unit_text.astype(bf16), image_all) * SCALE
    image_scores = dot_nt(image_all[:local_pairs], unit_all.astype(bf16)) * SCALE
    by_text, text_total = softmax_parts(text_scores, 1)
    image_total = softmax_parts(image_scores, 1)[1]
    every_total = gather_relative(image_total)
    own_same = own_rows(same)
    own = jnp.sum(text_scores * own_same, -1)
    pair_loss = 0.5 * (text_total[:, 0] - own) + 0.5 * (image_total[:, 0] - own)
    by_image = jnp.exp(text_scores - every_total[:, 0][None, :])
    sgrad = (0.5 * (by_text - own_same) + 0.5 * (by_image - own_same)).astype(bf16)
    grad_unit = dot(sgrad, image_all) * SCALE
    grads = branch_grad(grad_unit, unit_text, inverse_z, text_proj, own_rows(lengths_all))
    return pair_loss, grads, grads.astype(bf16)


def local(
    images,
    groups,
    captions,
    cap_lengths,
    img_gain_a,
    img_w_qkv,
    img_b_qv,
    img_w_out,
    img_gain_m,
    img_w_up,
    img_b_up,
    img_w_down,
    gain_attn,
    w_qkv,
    b_qv,
    w_out,
    gain_mlp,
    w_up,
    b_up,
    w_down,
    text_proj,
):
    local_pairs = images.shape[0]
    rows_total = local_pairs * CAP
    mine = lax.axis_index("rep").astype(jnp.int32)
    mine_one = mine[None]
    total_pairs = local_pairs * lax.axis_size("dp") * lax.axis_size("rep")
    whole = total_pairs <= MOST_PAIRS

    image_vec = jnp.concatenate([img_gain_a, img_b_qv, img_gain_m, img_b_up])[None]
    image_vec_other = swap(image_vec, "rep", 1)
    weights = []
    for weight in (img_w_qkv, img_w_out, img_w_up, img_w_down):
        weights += [weight, swap(weight, "rep", 1)]

    text_vec = jnp.concatenate([gain_attn, b_qv, gain_mlp, b_up]).astype(f32)[None]
    flat = captions.reshape(rows_total, D)
    qkv, mixed, after, mlp, slope, early, hidden_low = text_forward(
        flat, cap_lengths, text_vec, w_qkv, w_out, w_up, w_down
    )
    early_all = lax.all_gather(early, ("dp", "rep"), axis=0, tiled=True)
    if whole:
        hidden_all = lax.all_gather(hidden_low, ("dp", "rep"), axis=0, tiled=True)
    image_emb = image_tower(jnp.transpose(images, (1, 0, 2)), groups, mine_one, image_vec, image_vec_other, weights)
    image_all = gather_relative(image_emb)

    first_row = lax.axis_index(("dp", "rep")) * local_pairs
    chips = lax.axis_index("dp") ^ jnp.array(relative_chips(), jnp.int32)
    devices = jnp.concatenate([2 * chips + mine, 2 * chips + 1 - mine])
    image_ids = (
        devices[:, None] * local_pairs + jnp.arange(local_pairs, dtype=jnp.int32)[None, :]
    ).reshape(1, total_pairs)
    same = (jnp.arange(total_pairs, dtype=jnp.int32)[:, None] == image_ids).astype(f32)
    loss_of = loss_whole if whole else loss_rows
    pair_loss, grads, branch_all = loss_of(
        early_all[:, :D],
        image_all,
        text_proj,
        early_all[:, D : D + 1].astype(f32),
        same,
        first_row,
        local_pairs,
    )
    place = chunk_places()
    branch = grads.astype(bf16)
    grad_pre, up_own, up_other, grad_bup = up_backward(
        place, mine_one, cap_lengths, branch, slope, mlp, w_down
    )
    half = D // 2
    own_columns = lax.dynamic_slice_in_dim(branch_all, mine * half, half, 1)
    if whole:
        grad_w_down = dot_tn(hidden_all, own_columns)
    else:
        other_columns = lax.dynamic_slice_in_dim(branch_all, (1 - mine) * half, half, 1)
        grad_w_down = dot_tn(hidden_low, own_columns) + swap(
            dot_tn(hidden_low, other_columns).astype(bf16), "rep", 1
        ).astype(f32)
        grad_w_down = lax.psum(grad_w_down, "dp")
    up_chunk = reduce_chunks(up_own, swap(up_other, "rep", 1), FF // 4)
    grad_after, grad_mixed, grad_gain = mlp_backward(
        cap_lengths, grad_pre, grads, after, text_vec, w_up, w_out
    )
    low, high = (
        attention_backward(cap_lengths, qkv, grad_mixed, start, rows_total // 2)
        for start in (0, rows_total // 2)
    )
    caption_grad, rest_own, rest_other = proj_backward(
        place, mine_one, low, high, grad_after, mixed, flat, text_vec, grad_gain, grad_bup, w_qkv
    )
    rest_chunk = reduce_chunks(rest_own, swap(rest_other, "rep", 1), D)
    place, grad_w_down = lax.optimization_barrier((place, grad_w_down))
    grad_w_up, grad_w_qkv, grad_w_out, *small = unpack(
        place, spread_chunks(up_chunk, FF // 4), spread_chunks(rest_chunk, D)
    )
    return (
        pair_loss,
        caption_grad.reshape(local_pairs, CAP, D),
        small[0],
        grad_w_qkv,
        small[1],
        grad_w_out,
        small[2],
        grad_w_up,
        small[3],
        grad_w_down,
    )


def solution(mesh):
    in_specs = (
        P(("dp", "rep"), None, None),
        P(("dp", "rep")),
        P(("dp", "rep"), None, None),
        P(("dp", "rep")),
        P("rep"),
        P("rep", None),
        P("rep"),
        P("rep", None),
        P("rep"),
        P("rep", None),
        P("rep"),
        P("rep", None),
        P(),
        P(),
        P(),
        P(),
        P(),
        P(),
        P(),
        P(),
        P(),
    )
    out_specs = (
        P(("dp", "rep")),
        P(("dp", "rep"), None, None),
        P("rep"),
        P(None, "rep"),
        P("rep"),
        P(None, "rep"),
        P("rep"),
        P(None, "rep"),
        P("rep"),
        P(None, "rep"),
    )
    return jax.shard_map(local, mesh=mesh, in_specs=in_specs, out_specs=out_specs, check_vma=False)
```

time: 1710 us -> 399 us (0.23)
  waiting for transfers between devices: 670 us -> 81.8 us
  matrix products: 381 us -> 28.6 us
  local copies, waits for them, and re-layouts: 347 us -> 9.32 us
  Pallas kernels: 0 us -> 151 us
  other arithmetic: 165 us -> 20 us
  blocking collectives: 85.9 us -> 0 us
  starting transfers between devices: 0.74 us -> 85.8 us
  loops' own time: 47.3 us -> 0 us
    dot_general x61 -> x5, matrix products: 341 us -> 28.6 us  [the longest x2 13.1 us: dot_nt(): lax.dot_general(left_side, right_side, (((1,), (1,)), ((), ())), preferre...]
    psum x1 -> x0, waiting for transfers between devices: 303 us -> none  [local(): lax.psum((half_gain_a, half_qkv, half_bqv, half_out, half_gain_m, half_up...]
    all_gather x6 -> x2, waiting for transfers between devices: 225 us -> 0.01 us  [the longest x1 0.01 us: local(): early_all = lax.all_gather(early, ('dp', 'rep'), axis=0, tiled=True)]
    pallas_call x0 -> x8, Pallas kernels: none -> 151 us  [the longest x1 52.2 us: image_tower(): pl.pallas_call(tower_kernel, out_shape=jax.ShapeDtypeStruct((number, D),...]
    reduce_scatter x5 -> x0, waiting for transfers between devices: 139 us -> none  [the longest x1 101 us: local(): lax.psum_scatter(contract(image_sgrad, image_emb, 0, 0) * SCALE, ('dp', '...]
    reshape x28 -> x0, local copies, waits for them, and re-layouts: 109 us -> none  [the longest x9 56.6 us: block_forward(): projected = projected.reshape(number, span_len, 3, HEADS, head_dim)]
    ppermute x0 -> x46, starting transfers between devices: none -> 85.7 us  [swap(): lax.ppermute(values, axis, [(place, place ^ bit) for place in range(size)])]
    ppermute x0 -> x46, waiting for transfers between devices: none -> 81.7 us  [swap(): lax.ppermute(values, axis, [(place, place ^ bit) for place in range(size)])]
  transfers between devices with their start and end apart: 12 -> 48, of which waited for: 5 -> 19; matrix products, arithmetic and copies ran while one was open for 49% -> 14% of each run, Pallas kernels for 0% -> 37%
where the time goes in v2:
time: 399 us; the launch traced here: 392 us
  Pallas kernels  151 us (38%)
  starting transfers between devices  85.8 us (22%)
  waiting for transfers between devices  81.8 us (21%)
  matrix products  28.6 us (7%)
  other arithmetic  20 us (5%)
  between operations  15.2 us (4%)
  local copies, waits for them, and re-layouts  9.32 us (2%)
    ppermute x46, starting transfers between devices, swap(): lax.ppermute(values, axis, [(place, place ^ bit) for place in range(size)])  85.7 us
    ppermute x46, waiting for transfers between devices, swap(): lax.ppermute(values, axis, [(place, place ^ bit) for place in range(size)])  81.7 us
    pallas_call x1, Pallas kernels, image_tower(): pl.pallas_call(tower_kernel, out_shape=jax.ShapeDtypeStruct((number, D),...  52.2 us
    pallas_call x2, Pallas kernels, attention_backward(): pl.pallas_call(functools.partial(attention_kernel, start=start), out_shap...  28.4 us
    pallas_call x1, Pallas kernels, text_forward(): pl.pallas_call(forward_kernel, out_shape=[shape((rows, 3 * D), bf16), sha...  27.4 us
    pallas_call x1, Pallas kernels, proj_backward(): pl.pallas_call(proj_kernel, out_shape=[shape((rows, D), f32), shape((D, B...  13.7 us
    dot_general x2, matrix products, dot_nt(): lax.dot_general(left_side, right_side, (((1,), (1,)), ((), ())), preferre...  13.1 us
    pallas_call x1, Pallas kernels, up_backward(): pl.pallas_call(up_kernel, out_shape=[shape((rows, FF), bf16), shape((D, F...  12.8 us
  transfers between devices with their start and end apart: 48, of which 19 were waited for; matrix products, arithmetic and copies ran while one was open for 14% of the time, Pallas kernels for 37%

profile of v2, /device:TPU:8, one launch (start us, length us, event | category | flops | bytes accessed | tf_op | source)
XLA Modules:
  0.0 391.9 jit_solution(13270797642700440029)
XLA Ops:
  12.6 27.4 %text_forward.1 = (bf16[512,2304]{1,0:T(8,128)(2,1)}, bf16[512,768]{1,0:T(8,128)(2,1)}, f32[512,768]{1,0:T(8,128)}, bf16[512,768]{1,0:T(8,128)(2,1)}, bf16[512,3...) custom-call(s32[32]{0:T(128)} %lens_ref.9, bf16[512,768]{1,0:T(8,128)(2,1)} %bitcast.20, ...), custom_call_target="tpu_custom_call" | custom-call | flops 7247757312 | bytes 25165824 | tf_op jit(solution)/shard_map/text_forward/pallas_call | solution.py:484
  41.5 52.2 %image_tower.1 = bf16[32,768]{1,0:T(8,128)(2,1)} custom-call(s32[32]{0:T(128)} %groups_ref.1, s32[1]{0:T(128)} %bitcast.1.mine_ref, bf16[145,32,768]{2,1,0:T(8,128)(2,1)} %bitcast.19, bf16[1,3072]{1,0:T(2,128)(2,1)} %copy-done.15, bf16[1,3072]{1,0:T(2,128)(2,1)} %collective-permute-done.vec_other_ref, bf16[384,2304]{1,0:T(8,128)(2,1)} %qkv_own.1, ...), custom_call_target="tpu_custom_call" | custom-call | flops 30198988800 | bytes 25165824 | tf_op jit(solution)/shard_map/image_tower/pallas_call | solution.py:344
  93.7 26.9 %collective-permute-start.7 = (bf16[32,768]{1,0:T(8,128)(2,1)}, bf16[32,768]{1,0:T(8,128)(2,1)S(1)}, u32[]{:S(2)}, u32[]{:S(2)}) collective-permute-start(bf16[32,768]{1,0:T(8,128)(2,1)} %image_tower.1), channel_id=1, source_target_pairs={{0,24},{2,26},{4,28},{6,30},{8,16},{10,18},{12,20},{14,22},{16,8},... | collective-permute-start | bytes 147464 | tf_op jit(solution)/shard_map/ppermute | solution.py:729
  130.3 5.6 %collective-permute-done.8 = bf16[128,768]{1,0:T(8,128)(2,1)S(1)} collective-permute-done((bf16[128,768]{1,0:T(8,128)(2,1)S(1)}, bf16[128,768]{1,0:T(8,128)(2,1)S(1)}, u32[]{:S(2)}, u32[]{:S(2)}) %collective-permute-start.8) | collective-permute-done | bytes 196640 | tf_op jit(solution)/shard_map/ppermute | solution.py:729
  136.0 9.3 %collective-permute-start.11 = (bf16[512,768]{1,0:T(8,128)(2,1)S(1)}, bf16[512,768]{1,0:T(8,128)(2,1)S(1)}, u32[]{:S(2)}, u32[]{:S(2)}) collective-permute-start(bf16[512,768]{1,0:T(8,128)(2,1)S(1)} %get-tuple-element.76), channel_id=1, source_target_pairs={{0,1},{1,0},{2,3},{3,2},{4,5},{5,4},{6,7},{7,6},{8,9},{9,8},{10,11... | collective-permute-start | bytes 2359304 | tf_op jit(solution)/shard_map/ppermute | solution.py:729
  159.6 11.1 %broadcast_divide_fusion = f32[1024,768]{1,0:T(8,128)S(1)} fusion(f32[1024]{0:T(1024)S(1)} %convert_reduce_fusion, bf16[768,768]{1,0:T(8,128)(2,1)S(1)} %copy-done, f32[1024,768]{0,1:T(8,128)S(1)} %get-tuple-element.104, f32[1024,768]{0,1:T(8,128)S(1)} %get-tuple-element.101, f32[1024]{0:T(1024)S(1)} %get-tuple-element.103, f32[1024]{0:T(1024)S(1)} %add_rsqrt_fusion), kind=kOutput, calls=%fused_computation.20 | convolution fusion | flops 1213464576 | bytes 10629120 | tf_op jit(solution)/shard_map/dot_general | solution.py:43
  173.1 12.8 %up_backward.1 = (bf16[512,3072]{1,0:T(8,128)(2,1)}, f32[768,1536]{1,0:T(8,128)}, bf16[768,1536]{1,0:T(8,128)(2,1)}, f32[1,3072]{1,0:T(1,128)}) custom-call(s32[2,16]{1,0:T(2,128)} %pad_add_fusion.place_ref, s32[1]{0:T(128)} %bitcast.1.mine_ref, s32[32]{0:T(128)} %lens_ref.9, bf16[32,768]{1,0:T(8,128)(2,1)} %get-tuple-element.66.branch_ref, ...), custom_call_target="tpu_custom_call" | custom-call | flops 2415919104 | bytes 20971520 | tf_op jit(solution)/shard_map/up_backward/pallas_call | solution.py:547
  186.2 10.0 %mlp_backward.1 = (f32[512,768]{1,0:T(8,128)}, bf16[512,768]{1,0:T(8,128)(2,1)}, f32[1,768]{1,0:T(1,128)}) custom-call(s32[32]{0:T(128)} %lens_ref.9, bf16[512,3072]{1,0:T(8,128)(2,1)} %get-tuple-element.40.pre_ref, f32[32,768]{1,0:T(8,128)} %get-tuple-element.67.grad_ref, f32[512,768]{1,0:T(8,128)} %get-tuple-element.41.after_ref, ...), custom_call_target="tpu_custom_call" | custom-call | flops 3019898880 | bytes 20971520 | tf_op jit(solution)/shard_map/mlp_backward/pallas_call | solution.py:589
  196.2 14.1 %attention_backward.3.proj_high = bf16[256,2304]{1,0:T(8,128)(2,1)} custom-call(s32[32]{0:T(128)} %lens_ref.9, bf16[512,2304]{1,0:T(8,128)(2,1)} %get-tuple-element.37.qkv_ref, bf16[512,768]{1,0:T(8,128)(2,1)} %get-tuple-element.42.mixed_ref), custom_call_target="tpu_custom_call" | custom-call | flops 905969664 | bytes 16777216 | tf_op jit(solution)/shard_map/attention_backward/pallas_call | solution.py:640
  210.3 14.3 %attention_backward.2.proj_low = bf16[256,2304]{1,0:T(8,128)(2,1)} custom-call(s32[32]{0:T(128)} %lens_ref.9, bf16[512,2304]{1,0:T(8,128)(2,1)} %get-tuple-element.37.qkv_ref, bf16[512,768]{1,0:T(8,128)(2,1)} %get-tuple-element.42.mixed_ref), custom_call_target="tpu_custom_call" | custom-call | flops 905969664 | bytes 16777216 | tf_op jit(solution)/shard_map/attention_backward/pallas_call | solution.py:640
  224.5 13.7 %proj_backward.1 = (f32[512,768]{1,0:T(8,128)}, f32[768,1664]{1,0:T(8,128)}, bf16[768,1664]{1,0:T(8,128)(2,1)}) custom-call(s32[2,16]{1,0:T(2,128)} %pad_add_fusion.place_ref, s32[1]{0:T(128)} %bitcast.1.mine_ref, bf16[256,2304]{1,0:T(8,128)(2,1)} %attention_backward.2.proj_low, bf16[256,2304]{1,0:T(8,128)(2,1)} %attention_backward.3.proj_high, ...), custom_call_target="tpu_custom_call" | custom-call | flops 4227858432 | bytes 20971520 | tf_op jit(solution)/shard_map/proj_backward/pallas_call | solution.py:700
  248.0 9.3 %collective-permute-done.15 = bf16[384,768]{1,0:T(8,128)(2,1)S(1)} collective-permute-done((bf16[384,768]{1,0:T(8,128)(2,1)S(1)}, bf16[384,768]{1,0:T(8,128)(2,1)S(1)}, u32[]{:S(2)}, u32[]{:S(2)}) %collective-permute-start.15) | collective-permute-done | bytes 589856 | tf_op jit(solution)/shard_map/ppermute | solution.py:729
  264.2 7.7 %collective-permute-done.32 = bf16[384,896]{1,0:T(8,128)(2,1)S(1)} collective-permute-done((bf16[384,896]{1,0:T(8,128)(2,1)S(1)}, bf16[384,896]{1,0:T(8,128)(2,1)S(1)}, u32[]{:S(2)}, u32[]{:S(2)}) %collective-permute-start.32) | collective-permute-done | bytes 688160 | tf_op jit(solution)/shard_map/ppermute | solution.py:729
  274.2 3.6 collective-permute-done.31
  277.9 9.6 %collective-permute-done.33 = bf16[192,896]{1,0:T(8,128)(2,1)S(1)} collective-permute-done((bf16[192,896]{1,0:T(8,128)(2,1)S(1)}, bf16[192,896]{1,0:T(8,128)(2,1)S(1)}, u32[]{:S(2)}, u32[]{:S(2)}) %collective-permute-start.33) | collective-permute-done | bytes 344096 | tf_op jit(solution)/shard_map/ppermute | solution.py:729
  295.1 5.8 %collective-permute-done.36 = bf16[48,1664]{1,0:T(8,128)(2,1)S(1)} collective-permute-done((bf16[48,1664]{1,0:T(8,128)(2,1)S(1)}, bf16[48,1664]{1,0:T(8,128)(2,1)S(1)}, u32[]{:S(2)}, u32[]{:S(2)}) %collective-permute-start.36) | collective-permute-done | bytes 159776 | tf_op jit(solution)/shard_map/ppermute | solution.py:729
  302.5 4.3 %collective-permute-start.38 = (bf16[48,1664]{1,0:T(8,128)(2,1)S(1)}, bf16[48,1664]{1,0:T(8,128)(2,1)S(1)}, u32[]{:S(2)}, u32[]{:S(2)}) collective-permute-start(bf16[48,1664]{1,0:T(8,128)(2,1)S(1)} %fusion.19), channel_id=1, source_target_pairs={{0,16},{2,18},{4,20},{6,22},{8,24},{10,26},{12,28},{14,30},{16,0},... | collective-permute-start | bytes 479240 | tf_op jit(solution)/shard_map/ppermute | solution.py:729
  310.8 4.6 %collective-permute-done.39 = bf16[48,1664]{1,0:T(8,128)(2,1)S(1)} collective-permute-done((bf16[48,1664]{1,0:T(8,128)(2,1)S(1)}, bf16[48,1664]{1,0:T(8,128)(2,1)S(1)}, u32[]{:S(2)}, u32[]{:S(2)}) %collective-permute-start.39) | collective-permute-done | bytes 159776 | tf_op jit(solution)/shard_map/ppermute | solution.py:729
  315.4 3.9 collective-permute-done.38
  323.0 5.2 %collective-permute-done.19 = bf16[48,1536]{1,0:T(8,128)(2,1)S(1)} collective-permute-done((bf16[48,1536]{1,0:T(8,128)(2,1)S(1)}, bf16[48,1536]{1,0:T(8,128)(2,1)S(1)}, u32[]{:S(2)}, u32[]{:S(2)}) %collective-permute-start.19) | collective-permute-done | bytes 147488 | tf_op jit(solution)/shard_map/ppermute | solution.py:729
  329.5 7.7 %collective-permute-done.22 = bf16[48,1536]{1,0:T(8,128)(2,1)S(1)} collective-permute-done((bf16[48,1536]{1,0:T(8,128)(2,1)S(1)}, bf16[48,1536]{1,0:T(8,128)(2,1)S(1)}, u32[]{:S(2)}, u32[]{:S(2)}) %collective-permute-start.22) | collective-permute-done | bytes 147488 | tf_op jit(solution)/shard_map/ppermute | solution.py:729
  338.7 5.3 %collective-permute-done.21 = bf16[48,1536]{1,0:T(8,128)(2,1)S(1)} collective-permute-done((bf16[48,1536]{1,0:T(8,128)(2,1)S(1)}, bf16[48,1536]{1,0:T(8,128)(2,1)S(1)}, u32[]{:S(2)}, u32[]{:S(2)}) %collective-permute-start.21) | collective-permute-done | bytes 147488 | tf_op jit(solution)/shard_map/ppermute | solution.py:729
  367.8 9.2 %fusion.16 = f32[3072,384]{1,0:T(8,128)} fusion(bf16[1024,3072]{1,0:T(8,128)(2,1)} %all-gather.5.cloned.1.call-done, f32[1024,768]{1,0:T(8,128)} %copy-done.16, s32[]{:T(128)S(6)} %select_n.83), kind=kOutput, calls=%fused_computation.41 | convolution fusion | flops 2415919104 | bytes 11796484 | tf_op jit(solution)/shard_map/dot_general | solution.py:49
  377.8 6.8 %unpack.1 = (f32[768,1536]{1,0:T(8,128)}, f32[768,1152]{1,0:T(8,128)}, f32[768,384]{1,0:T(8,128)}, f32[384]{0:T(512)}, f32[768]{0:T(1024)}, /*index=5*/f32[384]{0:T(512)}, f32[1536]{0:T(1024)}) custom-call(s32[2,16]{1,0:T(2,128)} %pad_add_fusion.place_ref, bf16[192,768]{1,0:T(8,128)(2,1)} %copy-done.5, bf16[192,768]{1,0:T(8,128)(2,1)} %collective-permute-done.23.refs_1_, ...), custom_call_target="tpu_custom_call" | custom-call | tf_op jit(solution)/shard_map/unpack/pallas_call | solution.py:837
  (197 shorter events, 96.5 us)
Async XLA Ops:
  7.2 140.9 %all-gather.3.cloned.1.call-start = ((), (), s32[]{:S(2)}) async-start(), calls=%async_computation | async-start | bytes 1892352 | tf_op jit(solution)/shard_map/all_gather | solution.py:957
  7.2 32.9 %collective-permute-start.3 = (bf16[384,3072]{1,0:T(8,128)(2,1)}, bf16[384,3072]{1,0:T(8,128)(2,1)S(1)}, u32[]{:S(2)}, u32[]{:S(2)}) collective-permute-start(bf16[384,3072]{1,0:T(8,128)(2,1)} %up_own.1), channel_id=1, source_target_pairs={{0,1},{1,0},{2,3},{3,2},{4,5},{5,4},{6,7},{7,6},{8,9},{9,8},{10,11... | collective-permute-start | bytes 7077896 | tf_op jit(solution)/shard_map/ppermute | solution.py:729
  7.3 32.8 %collective-permute-start.4 = (bf16[1536,768]{1,0:T(8,128)(2,1)}, bf16[1536,768]{1,0:T(8,128)(2,1)}, u32[]{:S(2)}, u32[]{:S(2)}) collective-permute-start(bf16[1536,768]{1,0:T(8,128)(2,1)} %down_own.1), channel_id=1, source_target_pairs={{0,1},{1,0},{2,3},{3,2},{4,5},{5,4},{6,7},{7,6},{8,9},{9,8},{10,11... | collective-permute-start | bytes 7077896 | tf_op jit(solution)/shard_map/ppermute | solution.py:729
  7.8 32.3 %collective-permute-start.1 = (bf16[384,2304]{1,0:T(8,128)(2,1)}, bf16[384,2304]{1,0:T(8,128)(2,1)}, u32[]{:S(2)}, u32[]{:S(2)}) collective-permute-start(bf16[384,2304]{1,0:T(8,128)(2,1)} %qkv_own.1), channel_id=1, source_target_pairs={{0,1},{1,0},{2,3},{3,2},{4,5},{5,4},{6,7},{7,6},{8,9},{9,8},{10,11... | collective-permute-start | bytes 5308424 | tf_op jit(solution)/shard_map/ppermute | solution.py:729
  8.7 31.4 %collective-permute-start = (bf16[1,3072]{1,0:T(2,128)(2,1)S(1)}, bf16[1,3072]{1,0:T(2,128)(2,1)}, u32[]{:S(2)}, u32[]{:S(2)}) collective-permute-start(bf16[1,3072]{1,0:T(2,128)(2,1)S(1)} %broadcast_in_dim.5.vec_own_ref), channel_id=1, source_target_pairs={{0,1},{1,0},{2,3},{3,2},{4,5},{5,4},{6,7},{7,6},{8,9},{9,8},{10,11... | collective-permute-start | bytes 18440 | tf_op jit(solution)/shard_map/ppermute | solution.py:729
  9.2 30.9 %collective-permute-start.2 = (bf16[384,768]{1,0:T(8,128)(2,1)}, bf16[384,768]{1,0:T(8,128)(2,1)}, u32[]{:S(2)}, u32[]{:S(2)}) collective-permute-start(bf16[384,768]{1,0:T(8,128)(2,1)} %out_own.1), channel_id=1, source_target_pairs={{0,1},{1,0},{2,3},{3,2},{4,5},{5,4},{6,7},{7,6},{8,9},{9,8},{10,11... | collective-permute-start | bytes 1769480 | tf_op jit(solution)/shard_map/ppermute | solution.py:729
  40.0 327.8 %all-gather.5.cloned.1.call-start = ((), (), s32[]{:S(2)}) async-start(), calls=%async_computation.1 | async-start | bytes 6488064 | tf_op jit(solution)/shard_map/all_gather | solution.py:959
  93.7 29.3 %collective-permute-start.7 = (bf16[32,768]{1,0:T(8,128)(2,1)}, bf16[32,768]{1,0:T(8,128)(2,1)S(1)}, u32[]{:S(2)}, u32[]{:S(2)}) collective-permute-start(bf16[32,768]{1,0:T(8,128)(2,1)} %image_tower.1), channel_id=1, source_target_pairs={{0,24},{2,26},{4,28},{6,30},{8,16},{10,18},{12,20},{14,22},{16,8},... | collective-permute-start | bytes 147464 | tf_op jit(solution)/shard_map/ppermute | solution.py:729
  185.8 53.4 %collective-permute-start.12 = (bf16[768,1536]{1,0:T(8,128)(2,1)}, bf16[768,1536]{1,0:T(8,128)(2,1)S(1)}, u32[]{:S(2)}, u32[]{:S(2)}) collective-permute-start(bf16[768,1536]{1,0:T(8,128)(2,1)} %get-tuple-element.51), channel_id=1, source_target_pairs={{0,1},{1,0},{2,3},{3,2},{4,5},{5,4},{6,7},{7,6},{8,9},{9,8},{10,11... | collective-permute-start | bytes 7077896 | tf_op jit(solution)/shard_map/ppermute | solution.py:729
  241.0 16.2 %collective-permute-start.15 = (bf16[384,768]{1,0:T(8,128)(2,1)S(1)}, bf16[384,768]{1,0:T(8,128)(2,1)S(1)}, u32[]{:S(2)}, u32[]{:S(2)}) collective-permute-start(bf16[384,768]{1,0:T(8,128)(2,1)S(1)} %add_convert_fusion.2), channel_id=1, source_target_pairs={{0,4},{2,6},{4,0},{6,2},{8,12},{10,14},{12,8},{14,10},{16,20},{18,... | collective-permute-start | bytes 1769480 | tf_op jit(solution)/shard_map/ppermute | solution.py:729
  245.0 16.4 %collective-permute-start.30 = (bf16[384,768]{1,0:T(8,128)(2,1)S(1)}, bf16[384,768]{1,0:T(8,128)(2,1)S(1)}, u32[]{:S(2)}, u32[]{:S(2)}) collective-permute-start(bf16[384,768]{1,0:T(8,128)(2,1)S(1)} %add_convert_fusion.1), channel_id=1, source_target_pairs={{0,2},{2,0},{4,6},{6,4},{8,10},{10,8},{12,14},{14,12},{16,18},{18,... | collective-permute-start | bytes 1769480 | tf_op jit(solution)/shard_map/ppermute | solution.py:729
  247.1 24.9 %collective-permute-start.32 = (bf16[384,896]{1,0:T(8,128)(2,1)S(1)}, bf16[384,896]{1,0:T(8,128)(2,1)S(1)}, u32[]{:S(2)}, u32[]{:S(2)}) collective-permute-start(bf16[384,896]{1,0:T(8,128)(2,1)S(1)} %add_convert_fusion), channel_id=1, source_target_pairs={{0,4},{2,6},{4,0},{6,2},{8,12},{10,14},{12,8},{14,10},{16,20},{18,... | collective-permute-start | bytes 2064392 | tf_op jit(solution)/shard_map/ppermute | solution.py:729
  260.1 32.0 %collective-permute-start.13 = (bf16[384,768]{1,0:T(8,128)(2,1)S(1)}, bf16[384,768]{1,0:T(8,128)(2,1)S(1)}, u32[]{:S(2)}, u32[]{:S(2)}) collective-permute-start(bf16[384,768]{1,0:T(8,128)(2,1)S(1)} %get-tuple-element.69), channel_id=1, source_target_pairs={{0,2},{2,0},{4,6},{6,4},{8,10},{10,8},{12,14},{14,12},{16,18},{18,... | collective-permute-start | bytes 1769480 | tf_op jit(solution)/shard_map/ppermute | solution.py:729
  302.5 16.8 %collective-permute-start.38 = (bf16[48,1664]{1,0:T(8,128)(2,1)S(1)}, bf16[48,1664]{1,0:T(8,128)(2,1)S(1)}, u32[]{:S(2)}, u32[]{:S(2)}) collective-permute-start(bf16[48,1664]{1,0:T(8,128)(2,1)S(1)} %fusion.19), channel_id=1, source_target_pairs={{0,16},{2,18},{4,20},{6,22},{8,24},{10,26},{12,28},{14,30},{16,0},... | collective-permute-start | bytes 479240 | tf_op jit(solution)/shard_map/ppermute | solution.py:729
  307.3 15.2 %collective-permute-start.17 = (bf16[48,1536]{1,0:T(8,128)(2,1)S(1)}, bf16[48,1536]{1,0:T(8,128)(2,1)S(1)}, u32[]{:S(2)}, u32[]{:S(2)}) collective-permute-start(bf16[48,1536]{1,0:T(8,128)(2,1)S(1)} %get-tuple-element.73), channel_id=1, source_target_pairs={{0,8},{2,10},{4,12},{6,14},{8,0},{10,2},{12,4},{14,6},{16,24},{18,... | collective-permute-start | bytes 442376 | tf_op jit(solution)/shard_map/ppermute | solution.py:729
  309.0 19.2 %collective-permute-start.19 = (bf16[48,1536]{1,0:T(8,128)(2,1)S(1)}, bf16[48,1536]{1,0:T(8,128)(2,1)S(1)}, u32[]{:S(2)}, u32[]{:S(2)}) collective-permute-start(bf16[48,1536]{1,0:T(8,128)(2,1)S(1)} %get-tuple-element.74), channel_id=1, source_target_pairs={{0,24},{2,26},{4,28},{6,30},{8,16},{10,18},{12,20},{14,22},{16,8},... | collective-permute-start | bytes 442376 | tf_op jit(solution)/shard_map/ppermute | solution.py:729
  319.4 31.8 %collective-permute-start.41 = (bf16[192,768]{1,0:T(8,128)(2,1)S(1)}, bf16[192,768]{1,0:T(8,128)(2,1)S(1)}, u32[]{:S(2)}, u32[]{:S(2)}) collective-permute-start(bf16[192,768]{1,0:T(8,128)(2,1)S(1)} %pad_maximum_fusion.5.refs_8_), channel_id=1, source_target_pairs={{0,2},{2,0},{4,6},{6,4},{8,10},{10,8},{12,14},{14,12},{16,18},{18,... | collective-permute-start | bytes 884744 | tf_op jit(solution)/shard_map/ppermute | solution.py:729
  319.9 33.8 %collective-permute-start.40 = (bf16[192,768]{1,0:T(8,128)(2,1)S(1)}, bf16[192,768]{1,0:T(8,128)(2,1)}, u32[]{:S(2)}, u32[]{:S(2)}) collective-permute-start(bf16[192,768]{1,0:T(8,128)(2,1)S(1)} %pad_maximum_fusion.5.refs_8_), channel_id=1, source_target_pairs={{0,4},{2,6},{4,0},{6,2},{8,12},{10,14},{12,8},{14,10},{16,20},{18,... | collective-permute-start | bytes 884744 | tf_op jit(solution)/shard_map/ppermute | solution.py:729
  322.5 32.8 %collective-permute-start.44 = (bf16[192,896]{1,0:T(8,128)(2,1)S(1)}, bf16[192,896]{1,0:T(8,128)(2,1)S(1)}, u32[]{:S(2)}, u32[]{:S(2)}) collective-permute-start(bf16[192,896]{1,0:T(8,128)(2,1)S(1)} %pad_maximum_fusion.2.refs_12_), channel_id=1, source_target_pairs={{0,4},{2,6},{4,0},{6,2},{8,12},{10,14},{12,8},{14,10},{16,20},{18,... | collective-permute-start | bytes 1032200 | tf_op jit(solution)/shard_map/ppermute | solution.py:729
  328.2 27.2 %collective-permute-start.43 = (bf16[192,896]{1,0:T(8,128)(2,1)S(1)}, bf16[192,896]{1,0:T(8,128)(2,1)S(1)}, u32[]{:S(2)}, u32[]{:S(2)}) collective-permute-start(bf16[192,896]{1,0:T(8,128)(2,1)S(1)} %pad_maximum_fusion.2.refs_12_), channel_id=1, source_target_pairs={{0,2},{2,0},{4,6},{6,4},{8,10},{10,8},{12,14},{14,12},{16,18},{18,... | collective-permute-start | bytes 1032200 | tf_op jit(solution)/shard_map/ppermute | solution.py:729
  355.3 21.7 %collective-permute-start.27 = (bf16[192,768]{1,0:T(8,128)(2,1)S(1)}, bf16[192,768]{1,0:T(8,128)(2,1)}, u32[]{:S(2)}, u32[]{:S(2)}) collective-permute-start(bf16[192,768]{1,0:T(8,128)(2,1)S(1)} %pad_maximum_fusion.4.refs_4_), channel_id=1, source_target_pairs={{0,4},{2,6},{4,0},{6,2},{8,12},{10,14},{12,8},{14,10},{16,20},{18,... | collective-permute-start | bytes 884744 | tf_op jit(solution)/shard_map/ppermute | solution.py:729
  355.4 21.6 %collective-permute-start.42 = (bf16[192,768]{1,0:T(8,128)(2,1)}, bf16[192,768]{1,0:T(8,128)(2,1)}, u32[]{:S(2)}, u32[]{:S(2)}) collective-permute-start(bf16[192,768]{1,0:T(8,128)(2,1)} %collective-permute-done.40.refs_9_), channel_id=1, source_target_pairs={{0,2},{2,0},{4,6},{6,4},{8,10},{10,8},{12,14},{14,12},{16,18},{18,... | collective-permute-start | bytes 884744 | tf_op jit(solution)/shard_map/ppermute | solution.py:729
  359.4 17.6 %collective-permute-start.45 = (bf16[192,896]{1,0:T(8,128)(2,1)S(1)}, bf16[192,896]{1,0:T(8,128)(2,1)S(1)}, u32[]{:S(2)}, u32[]{:S(2)}) collective-permute-start(bf16[192,896]{1,0:T(8,128)(2,1)S(1)} %collective-permute-done.43.refs_13_), channel_id=1, source_target_pairs={{0,4},{2,6},{4,0},{6,2},{8,12},{10,14},{12,8},{14,10},{16,20},{18,... | collective-permute-start | bytes 1032200 | tf_op jit(solution)/shard_map/ppermute | solution.py:729
  361.7 15.4 %collective-permute-start.25 = (bf16[192,768]{1,0:T(8,128)(2,1)}, bf16[192,768]{1,0:T(8,128)(2,1)}, u32[]{:S(2)}, u32[]{:S(2)}) collective-permute-start(bf16[192,768]{1,0:T(8,128)(2,1)} %collective-permute-done.23.refs_1_), channel_id=1, source_target_pairs={{0,2},{2,0},{4,6},{6,4},{8,10},{10,8},{12,14},{14,12},{16,18},{18,... | collective-permute-start | bytes 884744 | tf_op jit(solution)/shard_map/ppermute | solution.py:729
  (45 other events, 705.8 us)
Sparse Core Ops, SparseCore 0:
  40.1 56.2 all-gather.2
  145.4 69.5 all-gather.4
